TPU v7x, 256 devices: a whole 4x4x8 slice. The times are simulated.
256 devices in a mesh: box: 32 (over z, x_lo, core), face: 8 (over y, x_hi).
Axes of the slice: x: 4 (x_hi: 2, x_lo: 2; x = x_hi * 2 + x_lo), y: 4, z: 8, core: 2. Of those that a mesh axis runs over, the one named last changes fastest.
Arguments:
- leaf_maps: bfloat16 [2, 1, 32, 3, 512, 1536], P(None, None, 'box', None, 'face'), may hold values from -6 to 6
- w_first: bfloat16 [2, 1, 8192, 512], P(None, None, 'box'), may hold values from -0.01171875 to 0.01171875
- w_second: bfloat16 [2, 1, 4096, 512], P(None, None, 'box'), may hold values from -0.01171875 to 0.01171875
- skel_first: int32 [1, 16, 512], replicated, may hold values from 0 to 1023, as said below
- skel_second: int32 [1, 8, 512], replicated, may hold values from 0 to 1023, as said below
Outputs:
- grand_maps: bfloat16 [2, 1, 16384, 1536], P(None, None, ('box', 'face'))
Inputs may be any that keep to these rules, and one draw needn't show every extreme that they name: `skel_first`: each row holds 512 distinct indices, 0 and 1023 among them. `skel_second`: each row holds 512 distinct indices, 0 and 1023 among them.
All inputs are finite; a program needn't handle non-finite values.
Results may differ from a plain program's by a relative error of at most 0.0075.
Values may be sent and summed in bfloat16 or wider, within the bound.
A program may use at most 64 MiB of HBM per device.

v0:
```python
import jax
import jax.numpy as jnp
from jax import lax
from jax.sharding import Mesh
from jax.sharding import PartitionSpec as P

K = 512
FACE = ("face_0", "face_1")
BOX_FACE = ("box", "face_0", "face_1")


def gathered_by_axis(array, axes, dim):
    whole = array
    for number in range(len(axes) - 1, -1, -1):
        whole = lax.all_gather(whole, axes[number], axis=dim, tiled=True)
    return whole


def in_blocks(array, dim, count):
    before, after = (array.shape[:dim], array.shape[dim + 1 :])
    return jnp.moveaxis(array.reshape(*before, count, -1, *after), dim, 0)


def sum_at_owner(array, axis, dim):
    tiles = in_blocks(array, dim, lax.axis_size(axis))
    arrived = lax.all_to_all(tiles, axis, split_axis=0, concat_axis=0, tiled=True)
    return arrived.astype(jnp.float32).sum(axis=0)


def partner(array, axis, bit):
    return lax.ppermute(array, axis, [(i, i ^ 1 << bit) for i in range(lax.axis_size(axis))])


def complex_dot(left_op, right_op):

    def real_dot(first_op, second_op):
        return jnp.einsum("trk,tkc->trc", first_op, second_op, preferred_element_type=jnp.float32)

    real_part = real_dot(left_op[0], right_op[0]) - real_dot(left_op[1], right_op[1])
    imag_part = real_dot(left_op[0], right_op[1]) + real_dot(left_op[1], right_op[0])
    return jnp.stack([real_part, imag_part])


def skeleton_picker(skeleton):
    side_index = jnp.arange(2 * K, dtype=jnp.int32)
    return (side_index[None, :, None] == skeleton[:, None, :]).astype(jnp.bfloat16)


def select_columns(left_cols, right_cols, picker):
    end_cols = jnp.concatenate([left_cols[:, :, :, :K], right_cols[:, :, :, K : 2 * K]], axis=3)
    side_cols = jnp.concatenate([left_cols[:, :, :, 2 * K :], right_cols[:, :, :, 2 * K :]], axis=3)
    picked = jnp.einsum("ptrs,tsk->ptrk", side_cols, picker, preferred_element_type=jnp.float32)
    return jnp.concatenate([end_cols.astype(jnp.float32), picked], axis=3)


def merge_rows(rows_own, iface_own, iface_other, weight_inv, skeleton, parity):
    picker = skeleton_picker(skeleton)
    coupling = lax.dynamic_slice_in_dim(rows_own, (1 - parity) * K, K, 3)
    hidden = complex_dot(coupling, weight_inv).astype(jnp.bfloat16)
    nothing = jnp.zeros_like(rows_own)
    own_left = jnp.where(parity == 0, rows_own, nothing)
    own_right = jnp.where(parity == 1, rows_own, nothing)
    diagonal = select_columns(own_left, own_right, picker)
    left_iface = jnp.where(parity == 0, iface_own, iface_other)
    right_iface = jnp.where(parity == 0, iface_other, iface_own)
    chosen = select_columns(left_iface, right_iface, picker).astype(jnp.bfloat16)
    product = complex_dot(hidden, gathered_by_axis(chosen, FACE, 2))
    return (diagonal - product).astype(jnp.bfloat16)


def select_rows(candidates, cand_index, skeleton):
    picker = (skeleton[:, :, None] == cand_index[None, None, :]).astype(jnp.bfloat16)
    picked_rows = jnp.einsum(
        "tjr,ptrc->jptc", picker, candidates, preferred_element_type=jnp.float32
    )
    picked = sum_at_owner(picked_rows.astype(jnp.bfloat16).astype(jnp.bfloat16), FACE, 0)
    return jnp.transpose(picked, (1, 2, 0, 3)).astype(jnp.bfloat16)


def on_device(leaf_maps, w_first, w_second, skel_first, skel_second):
    box_index = lax.axis_index("box")
    face_index = lax.axis_index(FACE)
    face_rows = leaf_maps.shape[4]
    leaf_faces = leaf_maps[:, :, 0]
    parity_one = box_index % 2
    first_face = lax.dynamic_index_in_dim(leaf_faces, 2 * parity_one, 2, keepdims=False)
    second_face = lax.dynamic_index_in_dim(leaf_faces, 2 - parity_one, 2, keepdims=False)
    rows_one = jnp.concatenate([first_face, second_face], axis=2)
    iface_one = lax.dynamic_index_in_dim(leaf_faces, 1 - parity_one, 2, keepdims=False)
    iface_sibling, w_half = partner((iface_one, w_first), "box", 0)
    w_one = jnp.where(
        parity_one == 0,
        jnp.concatenate([w_first, w_half], axis=2),
        jnp.concatenate([w_half, w_first], axis=2),
    )
    skel_one = lax.dynamic_index_in_dim(skel_first, box_index // 2, 1, keepdims=False)
    merged_one = merge_rows(rows_one, iface_one, iface_sibling, w_one, skel_one, parity_one)
    end_rows = jnp.where(
        parity_one == 0, merged_one[:, :, :face_rows], merged_one[:, :, face_rows:]
    )
    side_rows = jnp.where(
        parity_one == 0, merged_one[:, :, face_rows:], merged_one[:, :, :face_rows]
    )
    local_rows = face_index * face_rows + jnp.arange(face_rows, dtype=jnp.int32)
    own_pick = select_rows(side_rows, parity_one * K + local_rows, skel_one)
    end_other, pick_other, w_quarter = partner((end_rows, own_pick, w_second), "box", 0)
    side_parent = (own_pick.astype(jnp.float32) + pick_other.astype(jnp.float32)).astype(
        jnp.bfloat16
    )
    parity_two = box_index // 2 % 2
    quarter_role = box_index % 4
    w_pair = jnp.where(
        parity_one == 0,
        jnp.concatenate([w_second, w_quarter], axis=2),
        jnp.concatenate([w_quarter, w_second], axis=2),
    )
    iface_two = jnp.where(parity_one == 1 - parity_two, end_rows, end_other)
    rows_two = jnp.where((quarter_role == 1) | (quarter_role == 2), side_parent, end_rows)
    iface_cousin, w_cousin = partner((iface_two, w_pair), "box", 1)
    w_two = jnp.where(
        parity_two == 0,
        jnp.concatenate([w_pair, w_cousin], axis=2),
        jnp.concatenate([w_cousin, w_pair], axis=2),
    )
    skel_two = lax.dynamic_index_in_dim(skel_second, box_index // 4, 1, keepdims=False)
    return merge_rows(rows_two, iface_two, iface_cousin, w_two, skel_two, parity_two)


def solution(mesh):
    finer = Mesh(mesh.devices.reshape(mesh.shape["box"], 4, 2), ("box", "face_0", "face_1"))
    placed = (
        P(None, None, "box", None, FACE, None),
        P(None, None, "box", None),
        P(None, None, "box", None),
        P(),
        P(),
    )
    return jax.shard_map(
        on_device,
        mesh=finer,
        in_specs=placed,
        out_specs=P(None, None, BOX_FACE, None),
        check_vma=False,
    )
```

profile of v0, /device:TPU:1, one launch (start us, length us, event | category | flops | bytes accessed | tf_op | source)
XLA Modules:
  0.0 203.7 jit_solution(363313692275643255)
XLA Ops:
  6.5 0.0 copy-start
  6.5 1.3 dynamic-slice_bitcast_fusion
  7.9 3.3 %collective-permute-start.1 = (bf16[2,1,64,1536]{3,2,0,1:T(8,128)(2,1)S(1)}, bf16[2,1,64,1536]{3,2,0,1:T(8,128)(2,1)S(1)}, u32[]{:S(2)}, u32[]{:S(2)}) collective-permute-start(bf16[2,1,64,1536]{3,2,0,1:T(8,128)(2,1)S(1)} %get-tuple-element.8), channel_id=1, source_target_pairs={{0,8},{8,0},{16,24},{24,16},{32,40},{40,32},{48,56},{56,48},{64,72... | collective-permute-start | bytes 1179656 | tf_op jit(solution)/shard_map/ppermute | solution.py:31
  11.2 0.0 copy-done
  11.2 1.3 collective-permute-done.1
  12.5 0.1 broadcast_select_fusion.6
  12.6 0.0 copy-start.5
  12.6 0.5 fusion.33
  13.2 12.6 %all_gather.12 = bf16[2,1,128,1536]{3,2,0,1:T(8,128)(2,1)} all-gather(bf16[2,1,64,1536]{3,2,0,1:T(8,128)(2,1)S(1)} %pad_maximum_fusion.1), channel_id=1, replica_groups=mesh['box'=32,'face_0'=4,'face_1'=2] {'face_1'}, dimensions={2}, use_global_device_ids=true | all-gather | bytes 1179648 | tf_op jit(solution)/shard_map/all_gather | solution.py:15
  25.8 0.0 all-gather.3.cloned.1.call-update
  25.8 0.0 all-gather.5.cloned.1.call-start
  25.8 0.0 copy-done.5
  25.8 1.3 collective-permute-start
  27.2 0.2 broadcast_select_fusion.1
  27.4 0.1 slice_bitcast_fusion.24
  27.5 0.1 fusion.46
  27.6 0.5 fusion.19
  28.2 0.5 collective-permute-done
  28.7 0.4 maximum_select_fusion
  29.1 0.2 fusion.50
  29.4 0.2 fusion.51
  29.6 0.2 fusion.25
  29.8 0.2 fusion.26
  30.1 39.6 %all-gather.3.cloned.1.call-done = bf16[2,1,512,1536]{3,2,0,1:T(8,128)(2,1)} async-done(((bf16[2,1,128,1536]{3,2,0,1:T(8,128)(2,1)}), bf16[2,1,512,1536]{3,2,0,1:T(8,128)(2,1)}) %all-gather.3.cloned.1.call-update) | async-done | bytes 3145744 | tf_op jit(solution)/shard_map/all_gather | solution.py:15
  69.7 1.9 fusion.15
  71.6 1.8 fusion.16
  73.4 0.4 fusion
  73.8 0.4 fusion.1
  74.2 0.3 fusion.14
  74.5 1.1 convolution_convert_fusion
  75.6 0.3 copy.11
  75.9 43.8 %all_to_all.5 = bf16[8,64,2,1,1536]{4,1,2,3,0:T(8,128)(2,1)S(1)} all-to-all(bf16[8,64,2,1,1536]{4,1,2,3,0:T(8,128)(2,1)S(1)} %copy.11), channel_id=1, replica_groups=mesh['box'=32,'face_0'=4,'face_1'=2] {'face_0','face_1'}, dimensions={0} | all-to-all | bytes 6291456 | tf_op jit(solution)/shard_map/all_to_all | solution.py:26
  119.7 1.3 reduce_sum.12
  120.9 2.0 collective-permute-start.2
  122.9 1.6 collective-permute-done.2
  124.5 1.5 broadcast_select_fusion.9
  126.0 0.5 collective-permute-start.5
  126.4 1.3 collective-permute-done.5
  127.8 0.8 collective-permute-start.6
  128.6 0.7 constant_dynamic-slice_fusion
  129.3 8.9 %collective-permute-done.6 = bf16[2,1,64,1536]{3,2,0,1:T(8,128)(2,1)S(1)} collective-permute-done((bf16[2,1,64,1536]{3,2,0,1:T(8,128)(2,1)S(1)}, bf16[2,1,64,1536]{3,2,0,1:T(8,128)(2,1)S(1)}, u32[]{:S(2)}, u32[]{:S(2)}) %collective-permute-start.6) | collective-permute-done | bytes 393248 | tf_op jit(solution)/shard_map/ppermute | solution.py:31
  138.2 0.1 broadcast_select_fusion.8
  138.4 0.0 copy-start.4
  138.4 0.5 fusion.36
  138.9 11.7 %all_gather.14 = bf16[2,1,128,1536]{3,2,0,1:T(8,128)(2,1)} all-gather(bf16[2,1,64,1536]{3,2,0,1:T(8,128)(2,1)S(1)} %pad_maximum_fusion.2), channel_id=1, replica_groups=mesh['box'=32,'face_0'=4,'face_1'=2] {'face_1'}, dimensions={2}, use_global_device_ids=true | all-gather | bytes 1179648 | tf_op jit(solution)/shard_map/all_gather | solution.py:15
  150.6 0.0 all-gather.5.cloned.1.call-update
  150.7 2.2 %collective-permute-start.3 = (bf16[2,1,128,512]{3,2,1,0:T(8,128)(2,1)S(1)}, bf16[2,1,128,512]{3,2,1,0:T(8,128)(2,1)S(1)}, u32[]{:S(2)}, u32[]{:S(2)}) collective-permute-start(bf16[2,1,128,512]{3,2,1,0:T(8,128)(2,1)S(1)} %copy-done.4), channel_id=1, source_target_pairs={{0,8},{8,0},{16,24},{24,16},{32,40},{40,32},{48,56},{56,48},{64,72... | collective-permute-start | bytes 786440 | tf_op jit(solution)/shard_map/ppermute | solution.py:31
  152.8 1.2 collective-permute-done.3
  154.0 0.2 maximum_select_fusion.3
  154.2 0.8 collective-permute-start.4
  155.0 0.2 fusion.49
  155.2 12.3 %collective-permute-done.4 = bf16[2,1,256,512]{3,2,1,0:T(8,128)(2,1)S(1)} collective-permute-done((bf16[2,1,256,512]{3,2,1,0:T(8,128)(2,1)S(1)}, bf16[2,1,256,512]{3,2,1,0:T(8,128)(2,1)S(1)}, u32[]{:S(2)}, u32[]{:S(2)}) %collective-permute-start.4) | collective-permute-done | bytes 524320 | tf_op jit(solution)/shard_map/ppermute | solution.py:31
  167.5 0.4 maximum_select_fusion.1
  168.1 0.5 fusion.22
  168.6 0.2 fusion.52
  168.8 0.2 fusion.53
  169.0 0.2 fusion.39
  169.2 0.2 fusion.40
  169.4 22.1 %all-gather.5.cloned.1.call-done = bf16[2,1,512,1536]{3,2,0,1:T(8,128)(2,1)} async-done(((bf16[2,1,128,1536]{3,2,0,1:T(8,128)(2,1)}), bf16[2,1,512,1536]{3,2,0,1:T(8,128)(2,1)}) %all-gather.5.cloned.1.call-update) | async-done | bytes 3145744 | tf_op jit(solution)/shard_map/all_gather | solution.py:15
  191.5 1.9 fusion.17
  193.4 1.8 fusion.18
  195.2 0.4 fusion.2
  195.6 0.4 fusion.3
  196.0 0.8 fusion.55
  (23 shorter events, 0.4 us)
Async XLA Ops:
  6.5 4.6 %copy-start = (s32[1,16,512]{2,1,0:T(8,128)S(1)}, s32[1,16,512]{2,1,0:T(8,128)}, u32[]{:S(2)}) copy-start(s32[1,16,512]{2,1,0:T(8,128)} %param.8) | copy-start | bytes 98308
  6.5 63.1 %all-gather.3.cloned.1.call-start = ((), (), s32[]{:S(2)}) async-start(), calls=%async_computation.1 | async-start | bytes 3932160 | tf_op jit(solution)/shard_map/all_gather | solution.py:15
  7.9 4.6 %collective-permute-start.1 = (bf16[2,1,64,1536]{3,2,0,1:T(8,128)(2,1)S(1)}, bf16[2,1,64,1536]{3,2,0,1:T(8,128)(2,1)S(1)}, u32[]{:S(2)}, u32[]{:S(2)}) collective-permute-start(bf16[2,1,64,1536]{3,2,0,1:T(8,128)(2,1)S(1)} %get-tuple-element.8), channel_id=1, source_target_pairs={{0,8},{8,0},{16,24},{24,16},{32,40},{40,32},{48,56},{56,48},{64,72... | collective-permute-start | bytes 1179656 | tf_op jit(solution)/shard_map/ppermute | solution.py:31
  12.6 13.2 %copy-start.5 = (bf16[2,1,256,512]{3,2,1,0:T(8,128)(2,1)S(1)}, bf16[2,1,256,512]{3,2,1,0:T(8,128)(2,1)}, u32[]{:S(2)}) copy-start(bf16[2,1,256,512]{3,2,1,0:T(8,128)(2,1)} %param.6) | copy-start | bytes 1572868
  25.8 165.7 %all-gather.5.cloned.1.call-start = ((), (), s32[]{:S(2)}) async-start(), calls=%async_computation.2 | async-start | bytes 3932160 | tf_op jit(solution)/shard_map/all_gather | solution.py:15
  25.8 2.9 %collective-permute-start = (bf16[2,1,256,512]{3,2,1,0:T(8,128)(2,1)S(1)}, bf16[2,1,256,512]{3,2,1,0:T(8,128)(2,1)S(1)}, u32[]{:S(2)}, u32[]{:S(2)}) collective-permute-start(bf16[2,1,256,512]{3,2,1,0:T(8,128)(2,1)S(1)} %copy-done.5), channel_id=1, source_target_pairs={{0,8},{8,0},{16,24},{24,16},{32,40},{40,32},{48,56},{56,48},{64,72... | collective-permute-start | bytes 1572872 | tf_op jit(solution)/shard_map/ppermute | solution.py:31
  69.7 3.7 %copy-start.1 = (bf16[2,1,512,1536]{3,2,0,1:T(8,128)(2,1)S(1)}, bf16[2,1,512,1536]{3,2,0,1:T(8,128)(2,1)}, u32[]{:S(2)}) copy-start(bf16[2,1,512,1536]{3,2,0,1:T(8,128)(2,1)} %all-gather.3.cloned.1.call-done) | copy-start | bytes 9437188
  74.5 1.1 copy-start.3
  120.9 3.5 %collective-permute-start.2 = (bf16[2,1,64,1536]{3,2,0,1:T(8,128)(2,1)}, bf16[2,1,64,1536]{3,2,0,1:T(8,128)(2,1)S(1)}, u32[]{:S(2)}, u32[]{:S(2)}) collective-permute-start(bf16[2,1,64,1536]{3,2,0,1:T(8,128)(2,1)} %bitcast.180), channel_id=1, source_target_pairs={{0,8},{8,0},{16,24},{24,16},{32,40},{40,32},{48,56},{56,48},{64,72... | collective-permute-start | bytes 1179656 | tf_op jit(solution)/shard_map/ppermute | solution.py:31
  126.0 1.8 collective-permute-start.5
  127.8 10.4 %collective-permute-start.6 = (bf16[2,1,64,1536]{3,2,0,1:T(8,128)(2,1)S(1)}, bf16[2,1,64,1536]{3,2,0,1:T(8,128)(2,1)S(1)}, u32[]{:S(2)}, u32[]{:S(2)}) collective-permute-start(bf16[2,1,64,1536]{3,2,0,1:T(8,128)(2,1)S(1)} %broadcast_select_fusion.2), channel_id=1, source_target_pairs={{0,16},{8,24},{16,0},{24,8},{32,48},{40,56},{48,32},{56,40},{64,80... | collective-permute-start | bytes 1179656 | tf_op jit(solution)/shard_map/ppermute | solution.py:31
  138.4 12.3 %copy-start.4 = (bf16[2,1,128,512]{3,2,1,0:T(8,128)(2,1)S(1)}, bf16[2,1,128,512]{3,2,1,0:T(8,128)(2,1)}, u32[]{:S(2)}) copy-start(bf16[2,1,128,512]{3,2,1,0:T(8,128)(2,1)} %param.7) | copy-start | bytes 786436
  150.7 3.3 %collective-permute-start.3 = (bf16[2,1,128,512]{3,2,1,0:T(8,128)(2,1)S(1)}, bf16[2,1,128,512]{3,2,1,0:T(8,128)(2,1)S(1)}, u32[]{:S(2)}, u32[]{:S(2)}) collective-permute-start(bf16[2,1,128,512]{3,2,1,0:T(8,128)(2,1)S(1)} %copy-done.4), channel_id=1, source_target_pairs={{0,8},{8,0},{16,24},{24,16},{32,40},{40,32},{48,56},{56,48},{64,72... | collective-permute-start | bytes 786440 | tf_op jit(solution)/shard_map/ppermute | solution.py:31
  154.2 13.3 %collective-permute-start.4 = (bf16[2,1,256,512]{3,2,1,0:T(8,128)(2,1)S(1)}, bf16[2,1,256,512]{3,2,1,0:T(8,128)(2,1)S(1)}, u32[]{:S(2)}, u32[]{:S(2)}) collective-permute-start(bf16[2,1,256,512]{3,2,1,0:T(8,128)(2,1)S(1)} %maximum_select_fusion.3), channel_id=1, source_target_pairs={{0,16},{8,24},{16,0},{24,8},{32,48},{40,56},{48,32},{56,40},{64,80... | collective-permute-start | bytes 1572872 | tf_op jit(solution)/shard_map/ppermute | solution.py:31
  191.5 3.7 %copy-start.2 = (bf16[2,1,512,1536]{3,2,0,1:T(8,128)(2,1)S(1)}, bf16[2,1,512,1536]{3,2,0,1:T(8,128)(2,1)}, u32[]{:S(2)}) copy-start(bf16[2,1,512,1536]{3,2,0,1:T(8,128)(2,1)} %all-gather.5.cloned.1.call-done) | copy-start | bytes 9437188
Sparse Core Ops, SparseCore 0:
  25.9 43.7 all-gather.2
  150.8 40.6 all-gather.4
where the time goes:
time: 204 us
  waiting for transfers between devices  88.8 us (44%)
  blocking collectives  68.1 us (33%)
  matrix products  13.8 us (7%)
  between operations  13.8 us (7%)
  starting transfers between devices  10.8 us (5%)
  other arithmetic  5.91 us (3%)
  local copies, waits for them, and re-layouts  2.55 us (1%)
    all_gather x2, waiting for transfers between devices, gathered_by_axis(): whole = lax.all_gather(whole, axes[number], axis=dim, tiled=True)  61.6 us
    all_to_all x1, blocking collectives, sum_at_owner(): lax.all_to_all(tiles, axis, split_axis=0, concat_axis=0, tiled=True)  43.8 us
    ppermute x7, waiting for transfers between devices, partner(): lax.ppermute(array, axis, [(i, i ^ 1 << bit) for i in range(lax.axis_size...  27.1 us
    all_gather x2, blocking collectives, gathered_by_axis(): whole = lax.all_gather(whole, axes[number], axis=dim, tiled=True)  24.3 us
    ppermute x7, starting transfers between devices, partner(): lax.ppermute(array, axis, [(i, i ^ 1 << bit) for i in range(lax.axis_size...  10.8 us
    dot_general x16, matrix products, real_dot(): jnp.einsum('trk,tkc->trc', first_op, second_op, preferred_element_type=jn...  10.7 us
  transfers between devices with their start and end apart: 9, of which 9 were waited for; matrix products, arithmetic and copies ran while one was open for 3% of the time, Pallas kernels for 0%

commit v1 on v0

v1 whole, which is shorter than its diff:
```python
import functools

import jax
import jax.numpy as jnp
from jax import lax
from jax.experimental import pallas as pl
from jax.experimental.pallas import tpu as pltpu
from jax.sharding import PartitionSpec as P

K = 512
BF = jnp.bfloat16
F32 = jnp.float32
MESH = pl.DeviceIdType.MESH


def fdot(a, b):
    return jnp.dot(a, b, preferred_element_type=F32)


def remote(src, dst, send, recv, target):
    return pltpu.make_async_remote_copy(
        src_ref=src, dst_ref=dst, send_sem=send, recv_sem=recv, device_id=target, device_id_type=MESH
    )


def write_left(ref, real, imag):
    n = real.shape[0]
    ref[0:n, 0:K] = real
    ref[0:n, K : 2 * K] = -imag
    ref[n : 2 * n, 0:K] = imag
    ref[n : 2 * n, K : 2 * K] = real


class Spread:
    def __init__(self, buf, send, recv, dsend, drecv, b, f, c, fr):
        self.buf, self.send, self.recv, self.dsend, self.drecv = buf, send, recv, dsend, drecv
        self.c, self.fr, self.b = c, fr, b
        y, xh = f // 2, f % 2
        self.own = f
        self.up = ((y + 1) % 4) * 2 + xh
        self.down = ((y + 3) % 4) * 2 + xh
        self.far = ((y + 2) % 4) * 2 + xh
        self.side = y * 2 + (1 - xh)
        self.up_side = ((y + 1) % 4) * 2 + (1 - xh)
        self.down_side = ((y + 3) % 4) * 2 + (1 - xh)
        self.far_side = ((y + 2) % 4) * 2 + (1 - xh)
        half = fr // 2
        self.c0 = {
            0: (self.own, 0, self.up),
            1: (self.own, 1, self.down),
            2: (self.own, 0, self.side),
            3: (self.own, 1, self.up),
            4: (self.own, 0, self.down),
            5: (self.own, 1, self.side),
            6: (self.down, 0, self.up),
            7: (self.up, 1, self.down),
            8: (self.side, 0, self.up),
            9: (self.side, 0, self.down),
            10: (self.side, 1, self.up),
            11: (self.side, 1, self.down),
            12: (self.far, 0, self.side),
            13: (self.far, 1, self.side),
        }
        self.d0 = [
            (self.own, 0, fr),
            (self.down, 0, fr),
            (self.up, 0, fr),
            (self.side, 0, fr),
            (self.far, 0, half),
            (self.far, half, half),
            (self.down_side, 0, fr),
            (self.up_side, 0, fr),
            (self.far_side, 0, half),
            (self.far_side, half, half),
        ]

    def rows(self, face, at, n):
        return self.buf.at[pl.ds(pl.multiple_of(self.c * K + face * self.fr + at, 16), n), :]

    def hop(self, k):
        face, half, to = self.c0[k]
        view = self.rows(face, half * (self.fr // 2), self.fr // 2)
        return remote(view, view, self.send.at[k], self.recv.at[k], (self.b, to))

    def over(self, k):
        face, at, n = self.d0[k]
        view = self.rows(face, at, n)
        return remote(view, view, self.dsend.at[k], self.drecv.at[k], (self.b + 1 - 2 * self.c, self.own))

    def got(self, *ks):
        for k in ks:
            self.hop(k).wait_recv()

    def go(self, *ks):
        for k in ks:
            self.hop(k).start()

    def hand(self, *ks):
        for k in ks:
            self.over(k).start()

    def begin(self):
        self.go(0, 1, 2, 3, 4, 5)
        self.hand(0)

    def first(self):
        self.got(0)
        self.go(6)
        self.got(1)
        self.go(7)
        self.got(2)
        self.go(8, 9)
        self.got(3)
        self.hand(1)
        self.got(4)
        self.hand(2)
        self.got(5)
        self.go(10, 11)
        self.hand(3)

    def second(self):
        self.got(6)
        self.go(12)
        self.hand(4)
        self.got(7)
        self.go(13)
        self.hand(5)

    def third(self):
        self.got(8, 10)
        self.hand(6)
        self.got(9, 11)
        self.hand(7)
        self.got(12)
        self.hand(8)
        self.got(13)
        self.hand(9)

    def finish(self):
        for k in range(10):
            self.over(k).wait_recv()

    def drain(self):
        for k in range(14):
            self.hop(k).wait_send()
        for k in range(10):
            self.over(k).wait_send()


def kernel(fr, leaf, w1, w2, skel1, skel2, out, ifc, endr, xs, sel, srow, p1, p2, skt, wa, wb, ga, gb,
           lh, lh2, lhs_s, lh2_s, dp, dps, eb, r2, stg, ex, lsem, ssem, rsem, s1, r1, ds1, dr1, s2, r2s, ds2, dr2,
           asend, arecv, bsend, brecv):
    b, f = lax.axis_index("box"), lax.axis_index("face")
    c, h = b % 2, (b // 2) % 2
    q = b % 4
    sib = (b + 1 - 2 * c, f)
    inner_box = b + 2 - 4 * h
    inner, outer = (inner_box, f), (inner_box, f // 2 * 2 + 1 - f % 2)
    cross = (inner_box + 1 - 2 * c, f)
    mid = c != h

    barrier = pltpu.get_barrier_semaphore()
    peers = [(b, f ^ d) for d in range(1, 8)] + [(sib[0], f ^ d) for d in range(8)] + [inner, outer, cross]
    for peer in peers:
        pl.semaphore_signal(barrier, inc=1, device_id=peer, device_id_type=MESH)

    def local(k, src, dst):
        copy = pltpu.make_async_copy(src, dst, lsem.at[k])
        copy.start()
        return copy

    lw = 3 * 2 * K // 8
    loc_if = local(0, leaf.at[c, 0, 0, 1 - c], ifc.at[c])
    loc_end = local(1, leaf.at[:, 0, 0, c], endr)
    own_rows = pl.ds(pl.multiple_of(c * K + f * fr, 16), fr)

    def chunk_of(j):
        return leaf.at[j // 4, 0, 0, 2, :, pl.ds(pl.multiple_of(lw * (j % 4), 128), lw)]

    loc_xs = local(2, chunk_of(f), xs.at[own_rows, :])
    w1_rows = pl.ds(pl.multiple_of(c * (K // 2), 16), K // 2)
    w2_rows = pl.ds(pl.multiple_of(q * (K // 4), 16), K // 4)
    loc_w1 = local(3, w1.at[:, 0], wa.at[:, w1_rows, :])
    loc_w2 = local(4, w2.at[:, 0], wb.at[:, w2_rows, :])

    sk1 = skel1[0, pl.ds(b // 2, 1), :]
    sk2 = skel2[0, pl.ds(b // 4, 1), :]
    for part in range(4):
        at = part * 256
        index = lax.broadcasted_iota(jnp.int32, (256, K), 0) + at
        p1[at : at + 256, :] = jnp.where(index == sk1, 1.0, 0.0).astype(BF)
        p2[at : at + 256, :] = jnp.where(index == sk2, 1.0, 0.0).astype(BF)
    skt[...] = jnp.transpose(jnp.broadcast_to(sk1.astype(F32), (128, K)))

    pl.semaphore_wait(barrier, len(peers))

    t_if = remote(leaf.at[1 - c, 0, 0, 1 - c], ifc.at[c], ssem.at[0], rsem.at[0], sib)
    t_w1 = remote(w1.at[:, 0], wa.at[:, w1_rows, :], ssem.at[1], rsem.at[1], sib)
    t_w2 = remote(w2.at[:, 0], wb.at[:, w2_rows, :], ssem.at[2], rsem.at[2], sib)
    t_w2i = remote(w2.at[0, 0], wb.at[0, w2_rows, :], ssem.at[3], rsem.at[3], inner)
    t_w2o = remote(w2.at[1, 0], wb.at[1, w2_rows, :], ssem.at[4], rsem.at[4], outer)
    q2 = pl.ds(pl.multiple_of((q + 2 - 4 * h) * (K // 4), 16), K // 4)
    t_w2fi = remote(wb.at[0, q2, :], wb.at[0, q2, :], ssem.at[5], rsem.at[5], sib)
    t_w2fo = remote(wb.at[1, q2, :], wb.at[1, q2, :], ssem.at[6], rsem.at[6], sib)
    own_xs = pl.ds(pl.multiple_of(c * K, 16), K)
    t_xs = remote(xs.at[own_xs, :], xs.at[own_xs, :], ssem.at[7], rsem.at[7], sib)

    t_if.start()
    first_a = []
    for d in (7, 6, 5, 4, 3, 2, 1):
        copy = remote(chunk_of(f ^ d), xs.at[own_rows, :], asend.at[d - 1], arecv.at[d - 1], (b, f ^ d))
        copy.start()
        first_a.append(copy)
    t_w1.start()
    t_w2.start()

    ag1 = Spread(ga, s1, r1, ds1, dr1, b, f, c, fr)
    ag2 = Spread(gb, s2, r2s, ds2, dr2, b, f, c, fr)

    loc_if.wait()
    t_if.wait_recv()
    ga[own_rows, 0:K] = ifc[0, :, 0:K]
    ga[own_rows, K : 2 * K] = ifc[1, :, K : 2 * K]
    ga[own_rows, 2 * K :] = (
        fdot(ifc[0, :, 2 * K :], p1[0:K, :]) + fdot(ifc[1, :, 2 * K :], p1[K:, :])
    ).astype(BF)
    ag1.begin()

    def coupled(rows, side, left, left2, weights, pick, dest):
        couple = rows[:, :, pl.ds(pl.multiple_of((1 - side) * K, 128), K)]
        write_left(left, couple[0], couple[1])
        hid = fdot(left[...], weights[...].reshape(2 * K, K)).astype(BF)
        write_left(left2, hid[:fr], hid[fr:])
        side_cols = rows[:, :, 2 * K :].reshape(2 * fr, K)
        half = pick[pl.ds(pl.multiple_of(side * K, 16), K), :]
        dest[...] = fdot(side_cols, half).astype(BF)

    def merged(rows, side, left2, gathered, dest, block):
        prod = fdot(left2[...], gathered[:, block * K : (block + 1) * K])
        if block == 2:
            base = dest[...].astype(F32)
        else:
            on = jnp.where(side == block, 1.0, 0.0)
            base = rows[:, :, block * K : (block + 1) * K].reshape(2 * fr, K).astype(F32) * on
        return (base - prod).astype(BF).reshape(2, fr, K)

    loc_end.wait()
    loc_w1.wait()
    t_w1.wait_recv()
    coupled(endr, c, lh, lh2, wa, p1, dp)

    ag1.first()
    t_w2i.start()
    t_w2o.start()
    loc_xs.wait()
    for copy in first_a:
        copy.wait_recv()
    t_xs.start()
    ag1.second()

    t_xs.wait_recv()
    lane = lax.broadcasted_iota(jnp.int32, (256, 128), 1)
    mine = skt[pl.ds(pl.multiple_of(c * 256, 16), 256), :].astype(jnp.int32)
    total = None
    for part in range(8):
        hot = jnp.where(mine == lane + part * 128, 1.0, 0.0).astype(BF)
        term = fdot(hot, xs[part * 128 : (part + 1) * 128, :])
        total = term if total is None else total + term
    sel[...] = total.astype(BF)
    into = srow.at[f // 4, :, pl.ds(pl.multiple_of(lw * (f % 4), 128), lw)]
    dest_box = b - c + 1 - h
    for i in range(4):
        turn = (f + i) % 4
        src = sel.at[pl.ds(pl.multiple_of(turn * fr, 16), fr), :]
        copy = remote(src, into, bsend.at[i], brecv.at[f], (dest_box, 4 * c + turn))
        if i == 0:
            here = jnp.logical_and(f // 4 == c, mid)

            @pl.when(here)
            def _():
                pltpu.make_async_copy(src, into, brecv.at[f]).start()

            @pl.when(jnp.logical_not(here))
            def _():
                copy.start()
        else:
            copy.start()

    ag1.third()
    ag1.finish()

    for block in (2, 0, 1):
        eb[:, :, block * K : (block + 1) * K] = merged(endr, c, lh2, ga, dp, block)

    ex_own = [remote(stg.at[1 - c], ex.at[h], ssem.at[8], rsem.at[8], sib),
              remote(stg.at[1 - c], ex.at[h], ssem.at[9], rsem.at[9], cross),
              remote(stg.at[c], ex.at[h], ssem.at[10], rsem.at[10], inner)]

    @pl.when(mid)
    def _():
        stg[:, :, 0:K] = eb[:, :, pl.ds(pl.multiple_of(h * K, 128), K)]
        half = p2[pl.ds(pl.multiple_of(h * K, 16), K), :]
        stg[:, :, K:] = fdot(eb[:, :, 2 * K :].reshape(2 * fr, K), half).astype(BF).reshape(2, fr, K)
        for copy in ex_own:
            copy.start()
        ex[h] = stg[c]
        ex_own[1].wait_recv()

    @pl.when(jnp.logical_not(mid))
    def _():
        ex_own[0].wait_recv()
        ex_own[2].wait_recv()

    gb[own_rows, 0:K] = ex[0, :, 0:K]
    gb[own_rows, K : 2 * K] = ex[1, :, 0:K]
    gb[own_rows, 2 * K :] = ex[0, :, K:] + ex[1, :, K:]
    ag2.begin()

    @pl.when(mid)
    def _():
        for j in range(8):
            view = srow.at[j // 4, :, lw * (j % 4) : lw * (j % 4 + 1)]
            pltpu.make_async_copy(view, view, brecv.at[j]).wait()
        seen = skt[pl.ds(pl.multiple_of(f * fr, 16), fr), :]
        left1 = jnp.tile(jnp.where(seen < K, 1.0, 0.0), (1, 4)).astype(BF)
        right1 = 1 - left1
        left = jnp.concatenate([left1, left1], axis=0)
        right = 1 - left
        couple = [srow[t, :, K : 2 * K] * left1 + srow[t, :, 0:K] * right1 for t in range(2)]
        write_left(lhs_s, couple[0], couple[1])
        hid = fdot(lhs_s[...], wa[...].reshape(2 * K, K)).astype(BF)
        write_left(lh2_s, hid[:fr], hid[fr:])
        sides = srow[:, :, 2 * K :].reshape(2 * fr, K)
        dps[...] = (fdot(sides * left, p1[0:K, :]) + fdot(sides * right, p1[K:, :])).astype(BF)
        for block in (2, 0, 1):
            prod = fdot(lh2_s[...], ga[:, block * K : (block + 1) * K])
            if block == 2:
                base = dps[...].astype(F32)
            else:
                on = left if block == 0 else right
                base = (srow[:, :, block * K : (block + 1) * K].reshape(2 * fr, K) * on).astype(F32)
            r2[:, :, block * K : (block + 1) * K] = (base - prod).astype(BF).reshape(2, fr, K)

    @pl.when(jnp.logical_not(mid))
    def _():
        r2[...] = eb[...]

    ag2.first()
    t_w2i.wait_recv()
    t_w2fi.start()
    t_w2o.wait_recv()
    t_w2fo.start()
    ag2.second()
    loc_w2.wait()
    t_w2.wait_recv()
    t_w2fi.wait_recv()
    t_w2fo.wait_recv()
    coupled(r2, h, lh, lh2, wb, p2, dp)
    ag2.third()
    ag2.finish()
    for block in (0, 1, 2):
        out[:, 0, :, block * K : (block + 1) * K] = merged(r2, h, lh2, gb, dp, block)

    for copy in [t_if, t_w1, t_w2, t_w2i, t_w2o, t_w2fi, t_w2fo, t_xs] + first_a:
        copy.wait_send()
    for i in range(4):
        turn = (f + i) % 4
        src = sel.at[pl.ds(pl.multiple_of(turn * fr, 16), fr), :]
        copy = remote(src, into, bsend.at[i], brecv.at[f], (dest_box, 4 * c + turn))
        if i == 0:

            @pl.when(jnp.logical_not(here))
            def _():
                copy.wait_send()
        else:
            copy.wait_send()

    @pl.when(mid)
    def _():
        for copy in ex_own:
            copy.wait_send()

    ag1.drain()
    ag2.drain()


def on_device(leaf, w1, w2, skel1, skel2):
    fr = leaf.shape[4]
    any_spec = pl.BlockSpec(memory_space=pl.ANY)
    vmem_spec = pl.BlockSpec(memory_space=pltpu.VMEM)
    dma = pltpu.SemaphoreType.DMA
    lw = 3 * 2 * K // 8
    scratch = [
        pltpu.VMEM((2, fr, 3 * K), BF),
        pltpu.VMEM((2, fr, 3 * K), BF),
        pltpu.VMEM((2 * K, lw), BF),
        pltpu.VMEM((K // 2, lw), BF),
        pltpu.VMEM((2, fr, 3 * K), BF),
        pltpu.VMEM((2 * K, K), BF),
        pltpu.VMEM((2 * K, K), BF),
        pltpu.VMEM((K, 128), F32),
        pltpu.VMEM((2, K, K), BF),
        pltpu.VMEM((2, K, K), BF),
        pltpu.VMEM((2 * K, 3 * K), BF),
        pltpu.VMEM((2 * K, 3 * K), BF),
        pltpu.VMEM((2 * fr, 2 * K), BF),
        pltpu.VMEM((2 * fr, 2 * K), BF),
        pltpu.VMEM((2 * fr, 2 * K), BF),
        pltpu.VMEM((2 * fr, 2 * K), BF),
        pltpu.VMEM((2 * fr, K), BF),
        pltpu.VMEM((2 * fr, K), BF),
        pltpu.VMEM((2, fr, 3 * K), BF),
        pltpu.VMEM((2, fr, 3 * K), BF),
        pltpu.VMEM((2, fr, 2 * K), BF),
        pltpu.VMEM((2, fr, 2 * K), BF),
        dma((5,)),
        dma((11,)),
        dma((11,)),
        dma((14,)),
        dma((14,)),
        dma((10,)),
        dma((10,)),
        dma((14,)),
        dma((14,)),
        dma((10,)),
        dma((10,)),
        dma((7,)),
        dma((7,)),
        dma((4,)),
        dma((8,)),
    ]
    return pl.pallas_call(
        functools.partial(kernel, fr),
        out_shape=jax.ShapeDtypeStruct((2, 1, fr, 3 * K), BF),
        in_specs=[any_spec, any_spec, any_spec, vmem_spec, vmem_spec],
        out_specs=vmem_spec,
        scratch_shapes=scratch,
        compiler_params=pltpu.CompilerParams(
            collective_id=0, has_side_effects=True, vmem_limit_bytes=48 * 1024 * 1024
        ),
    )(leaf, w1, w2, skel1, skel2)


def solution(mesh):
    return jax.shard_map(
        on_device,
        mesh=mesh,
        in_specs=(
            P(None, None, "box", None, "face", None),
            P(None, None, "box", None),
            P(None, None, "box", None),
            P(),
            P(),
        ),
        out_specs=P(None, None, ("box", "face"), None),
        check_vma=False,
    )
```

time: 204 us -> 58.6 us (0.29)
  waiting for transfers between devices: 88.8 us -> 0 us
  blocking collectives: 68.1 us -> 0 us
  Pallas kernels: 0 us -> 52.8 us
  matrix products: 13.8 us -> 0 us
  between operations: 13.8 us -> 0.01 us
  starting transfers between devices: 10.8 us -> 0 us
  other arithmetic: 5.91 us -> 0 us
  local copies, waits for them, and re-layouts: 2.55 us -> 5.48 us
    all_gather x2 -> x0, waiting for transfers between devices: 61.6 us -> none  [gathered_by_axis(): whole = lax.all_gather(whole, axes[number], axis=dim, tiled=True)]
    pallas_call x0 -> x1, Pallas kernels: none -> 52.8 us  [on_device(): pl.pallas_call(functools.partial(kernel, fr), out_shape=jax.ShapeDtypeStr...]
    all_to_all x1 -> x0, blocking collectives: 43.8 us -> none  [sum_at_owner(): lax.all_to_all(tiles, axis, split_axis=0, concat_axis=0, tiled=True)]
    ppermute x7 -> x0, waiting for transfers between devices: 27.1 us -> none  [partner(): lax.ppermute(array, axis, [(i, i ^ 1 << bit) for i in range(lax.axis_size...]
    all_gather x2 -> x0, blocking collectives: 24.3 us -> none  [gathered_by_axis(): whole = lax.all_gather(whole, axes[number], axis=dim, tiled=True)]
    dot_general x21 -> x0, matrix products: 13.8 us -> none  [the longest x16 10.7 us: real_dot(): jnp.einsum('trk,tkc->trc', first_op, second_op, preferred_element_type=jn...]
    ppermute x7 -> x0, starting transfers between devices: 10.8 us -> none  [partner(): lax.ppermute(array, axis, [(i, i ^ 1 << bit) for i in range(lax.axis_size...]
    unnamed x12 -> x11, local copies, waits for them, and re-layouts: 0.03 us -> 5.48 us
  transfers between devices with their start and end apart: 9 -> 0, of which waited for: 9 -> 0; matrix products, arithmetic and copies ran while one was open for 3% -> 0% of each run, Pallas kernels for 0% -> 0%
where the time goes in v1:
time: 58.6 us; the launch traced here: 58.3 us
  Pallas kernels  52.8 us (90%)
  local copies, waits for them, and re-layouts  5.48 us (9%)
    pallas_call x1, Pallas kernels, on_device(): pl.pallas_call(functools.partial(kernel, fr), out_shape=jax.ShapeDtypeStr...  52.8 us
    unnamed x11, local copies, waits for them, and re-layouts  5.48 us

profile of v1, /device:TPU:1, one launch (start us, length us, event | category | flops | bytes accessed | tf_op | source)
XLA Modules:
  0.0 58.3 jit_solution(10248968499904312882)
XLA Ops:
  0.0 0.0 copy-start
  0.0 1.3 %copy-done = bf16[2,1,1,3,64,1536]{5,4,3,2,1,0:T(8,128)(2,1)S(1)} copy-done((bf16[2,1,1,3,64,1536]{5,4,3,2,1,0:T(8,128)(2,1)S(1)}, bf16[2,1,1,3,64,1536]{5,4,3,2,1,0:T(8,128)(2,1)}, u32[]{:S(2)}) %copy-start) | copy-done | bytes 1179672
  1.3 0.0 copy-start.1
  1.3 1.0 %copy-done.1 = bf16[2,1,256,512]{3,2,1,0:T(8,128)(2,1)S(1)} copy-done((bf16[2,1,256,512]{3,2,1,0:T(8,128)(2,1)S(1)}, bf16[2,1,256,512]{3,2,1,0:T(8,128)(2,1)}, u32[]{:S(2)}) %copy-start.1) | copy-done | bytes 524312
  2.3 0.0 copy-start.2
  2.3 0.9 %copy-done.2 = bf16[2,1,128,512]{3,2,1,0:T(8,128)(2,1)S(1)} copy-done((bf16[2,1,128,512]{3,2,1,0:T(8,128)(2,1)S(1)}, bf16[2,1,128,512]{3,2,1,0:T(8,128)(2,1)}, u32[]{:S(2)}) %copy-start.2) | copy-done | bytes 262168
  3.3 0.0 copy-start.3
  3.3 0.8 %copy-done.3 = s32[1,16,512]{2,1,0:T(8,128)S(1)} copy-done((s32[1,16,512]{2,1,0:T(8,128)S(1)}, s32[1,16,512]{2,1,0:T(8,128)}, u32[]{:S(2)}) %copy-start.3) | copy-done | bytes 32792
  4.0 0.0 copy-start.4
  4.0 0.7 %copy-done.4 = s32[1,8,512]{2,1,0:T(8,128)S(1)} copy-done((s32[1,8,512]{2,1,0:T(8,128)S(1)}, s32[1,8,512]{2,1,0:T(8,128)}, u32[]{:S(2)}) %copy-start.4) | copy-done | bytes 16408
  4.7 52.8 %shard_map.55 = bf16[2,1,64,1536]{3,2,1,0:T(8,128)(2,1)S(1)} custom-call(bf16[2,1,1,3,64,1536]{5,4,3,2,1,0:T(8,128)(2,1)S(1)} %copy-done, bf16[2,1,256,512]{3,2,1,0:T(8,128)(2,1)S(1)} %copy-done.1, bf16[2,1,128,512]{3,2,1,0:T(8,128)(2,1)S(1)} %copy-done.2, s32[1,16,512]{2,1,0:T(8,128)S(1)} %copy-done.3, s32[1,8,512]{2,1,0:T(8,128)S(1)} %copy-done.4), custom_call_target="tpu_custom_call" | custom-call | tf_op jit(solution)/shard_map/pallas_call | solution.py:432
  57.6 0.7 %copy.7 = bf16[2,1,64,1536]{3,2,1,0:T(8,128)(2,1)} copy(bf16[2,1,64,1536]{3,2,1,0:T(8,128)(2,1)S(1)} %shard_map.55) | data formatting | bytes 786432
Async XLA Ops:
  0.0 1.3 %copy-start = (bf16[2,1,1,3,64,1536]{5,4,3,2,1,0:T(8,128)(2,1)S(1)}, bf16[2,1,1,3,64,1536]{5,4,3,2,1,0:T(8,128)(2,1)}, u32[]{:S(2)}) copy-start(bf16[2,1,1,3,64,1536]{5,4,3,2,1,0:T(8,128)(2,1)} %leaf.1) | copy-start | bytes 3538948
  1.3 1.0 %copy-start.1 = (bf16[2,1,256,512]{3,2,1,0:T(8,128)(2,1)S(1)}, bf16[2,1,256,512]{3,2,1,0:T(8,128)(2,1)}, u32[]{:S(2)}) copy-start(bf16[2,1,256,512]{3,2,1,0:T(8,128)(2,1)} %w1.1) | copy-start | bytes 1572868
  2.3 0.9 %copy-start.2 = (bf16[2,1,128,512]{3,2,1,0:T(8,128)(2,1)S(1)}, bf16[2,1,128,512]{3,2,1,0:T(8,128)(2,1)}, u32[]{:S(2)}) copy-start(bf16[2,1,128,512]{3,2,1,0:T(8,128)(2,1)} %w2.1) | copy-start | bytes 786436
  3.3 0.8 %copy-start.3 = (s32[1,16,512]{2,1,0:T(8,128)S(1)}, s32[1,16,512]{2,1,0:T(8,128)}, u32[]{:S(2)}) copy-start(s32[1,16,512]{2,1,0:T(8,128)} %skel1.1) | copy-start | bytes 98308
  4.0 0.7 %copy-start.4 = (s32[1,8,512]{2,1,0:T(8,128)S(1)}, s32[1,8,512]{2,1,0:T(8,128)}, u32[]{:S(2)}) copy-start(s32[1,8,512]{2,1,0:T(8,128)} %skel2.1) | copy-start | bytes 49156

commit v2 on v1

v2 whole, which is shorter than its diff:
```python
import functools

import jax
import jax.numpy as jnp
from jax import lax
from jax.experimental import pallas as pl
from jax.experimental.pallas import tpu as pltpu
from jax.sharding import PartitionSpec as P

K = 512
BF = jnp.bfloat16
F32 = jnp.float32
MESH = pl.DeviceIdType.MESH
ROWS_A = 48
EARLY = (3, 5, 7)


def fdot(a, b):
    return jnp.dot(a, b, preferred_element_type=F32)


def remote(src, dst, send, recv, target):
    return pltpu.make_async_remote_copy(
        src_ref=src, dst_ref=dst, send_sem=send, recv_sem=recv, device_id=target, device_id_type=MESH
    )


def write_left(ref, real, imag):
    n = real.shape[0]
    ref[0:n, 0:K] = real
    ref[0:n, K : 2 * K] = -imag
    ref[n : 2 * n, 0:K] = imag
    ref[n : 2 * n, K : 2 * K] = real


class Gather:
    def __init__(self, view, send, recv, dsend, drecv, sib):
        self.view, self.send, self.recv, self.dsend, self.drecv, self.sib = view, send, recv, dsend, drecv, sib
        self.hops, self.hands = [], []

    def hop(self, k):
        what, to = self.hops[k]
        ref = self.view(*what)
        return remote(ref, ref, self.send.at[k], self.recv.at[k], to)

    def hand_over(self, k):
        ref = self.view(*self.hands[k])
        return remote(ref, ref, self.dsend.at[k], self.drecv.at[k], self.sib)

    def got(self, *ks):
        for k in ks:
            self.hop(k).wait_recv()

    def go(self, *ks):
        for k in ks:
            self.hop(k).start()

    def hand(self, *ks):
        for k in ks:
            self.hand_over(k).start()

    def handed(self):
        for k in range(len(self.hands)):
            self.hand_over(k).wait_recv()

    def drain(self):
        for k in range(len(self.hops)):
            self.hop(k).wait_send()
        for k in range(len(self.hands)):
            self.hand_over(k).wait_send()


def face_gather(view, sems, b, f, sib, fr):
    g = Gather(view, *sems, sib)
    y, xh = f // 2, f % 2

    def at(dy, dx):
        return ((y + dy) % 4) * 2 + (xh + dx) % 2

    own, up, down, far = at(0, 0), at(1, 0), at(3, 0), at(2, 0)
    side, up_side, down_side, far_side = at(0, 1), at(1, 1), at(3, 1), at(2, 1)
    first, last, every = (0, ROWS_A), (ROWS_A, fr - ROWS_A), (0, fr)
    lo, hi, full = (0, 3 * K // 2), (3 * K // 2, 3 * K // 2), (0, 3 * K)
    x, u, d = (b, side), (b, up), (b, down)
    g.hops = [
        ((own, first, full), x),
        ((own, last, full), u),
        ((own, last, full), d),
        ((own, first, full), u),
        ((own, first, full), d),
        ((own, last, full), x),
        ((down, last, lo), u),
        ((up, last, hi), d),
        ((down, last, full), x),
        ((up, last, full), x),
        ((side, first, full), u),
        ((side, first, full), d),
        ((far, last, lo), x),
        ((far, last, hi), x),
        ((down, first, lo), u),
        ((up, first, hi), d),
        ((down_side, first, lo), u),
        ((up_side, first, hi), d),
    ]
    g.hands = [
        (own, every, full),
        (side, first, full),
        (down, every, full),
        (up, every, full),
        (far, last, full),
        (far, first, full),
        (side, last, full),
        (down_side, first, full),
        (up_side, first, full),
        (down_side, last, full),
        (up_side, last, full),
        (far_side, last, full),
        (far_side, first, full),
    ]
    return g


def plane_gather(view, sems, b, f, h, cross_box, sib, fr):
    g = Gather(view, *sems, sib)
    y, xh = f // 2, f % 2

    def face(dy, dx):
        return ((y + dy) % 4) * 2 + (xh + dx) % 2

    xs = [(h, 0), (1 - h, 0), (1 - h, 1), (h, 1)]
    ys = [0, 1, 3, 2]

    def node(iy, ix):
        return (xs[ix][0], face(ys[iy], xs[ix][1]))

    alpha, beta, every = (0, fr // 2), (fr // 2, fr // 2), (0, fr)
    lo, hi, full = (0, K // 2), (K // 2, K // 2), (0, K)
    inner, outer = (cross_box, f), (cross_box, face(0, 1))
    up, down = (b, face(1, 0)), (b, face(3, 0))
    g.hops += [
        ((node(0, 0), alpha, full), inner),
        ((node(0, 0), alpha, full), outer),
        ((node(0, 1), alpha, lo), outer),
        ((node(0, 2), alpha, hi), inner),
    ]
    g.hops += [
        ((node(0, 0), beta, full), up),
        ((node(0, 0), beta, full), down),
        ((node(2, 0), beta, lo), up),
        ((node(1, 0), beta, hi), down),
    ]
    for i in range(4):
        g.hops += [
            ((node(0, i), alpha, full), up),
            ((node(0, i), alpha, full), down),
            ((node(2, i), alpha, lo), up),
            ((node(1, i), alpha, hi), down),
        ]
    for i in range(4):
        g.hops += [
            ((node(i, 0), beta, full), inner),
            ((node(i, 0), beta, full), outer),
            ((node(i, 1), beta, lo), outer),
            ((node(i, 2), beta, hi), inner),
        ]
    g.hands = [(node(i // 4, i % 4), every, full) for i in range(16)]
    return g


def kernel(fr, leaf, w1, w2, skel1, skel2, out, sk1v, sk2v, ifc, endr, xs, sel, srow, p1, p2, skt, wa, wb, ga, gt,
           lh, lh2, lhs_s, lh2_s, dp, dps, r2, stg, pex, res, lsem, ssem, rsem, s1, r1, ds1, dr1, s2, r2s, ds2, dr2,
           asend, arecv, bsend, brecv):
    b, f = lax.axis_index("box"), lax.axis_index("face")
    c, h = b % 2, (b // 2) % 2
    q = b % 4
    sib = (b + 1 - 2 * c, f)
    inner_box = b + 2 - 4 * h
    other_face = f // 2 * 2 + 1 - f % 2
    inner, outer = (inner_box, f), (inner_box, other_face)
    cross_box = inner_box + 1 - 2 * c
    mid = c != h

    barrier = pltpu.get_barrier_semaphore()
    peers = [(b, f ^ d) for d in range(1, 8)] + [(sib[0], f ^ d) for d in range(8)]
    peers += [inner, outer, (cross_box, f), (cross_box, other_face)]
    for peer in peers:
        pl.semaphore_signal(barrier, inc=1, device_id=peer, device_id_type=MESH)

    def local(k, src, dst):
        copy = pltpu.make_async_copy(src, dst, lsem.at[k])
        copy.start()
        return copy

    loc_s1 = local(5, skel1, sk1v)
    loc_s2 = local(6, skel2, sk2v)
    lw = 3 * 2 * K // 8
    loc_if = local(0, leaf.at[c, 0, 0, 1 - c], ifc.at[c])
    loc_end = local(1, leaf.at[:, 0, 0, c], endr)
    own_rows = pl.ds(pl.multiple_of(c * K + f * fr, 16), fr)
    face_rows = pl.ds(pl.multiple_of(f * fr, 16), fr)

    def chunk_of(j):
        return leaf.at[j // 4, 0, 0, 2, :, pl.ds(pl.multiple_of(lw * (j % 4), 128), lw)]

    loc_xs = local(2, chunk_of(f), xs.at[own_rows, :])
    w1_rows = pl.ds(pl.multiple_of(c * (K // 2), 16), K // 2)
    w2_rows = pl.ds(pl.multiple_of(q * (K // 4), 16), K // 4)
    loc_w1 = local(3, w1.at[:, 0], wa.at[:, w1_rows, :])
    loc_w2 = local(4, w2.at[:, 0], wb.at[:, w2_rows, :])

    loc_s1.wait()
    loc_s2.wait()
    sk1 = sk1v[0, pl.ds(b // 2, 1), :]
    sk2 = sk2v[0, pl.ds(b // 4, 1), :]
    for part in range(4):
        at = part * 256
        index = lax.broadcasted_iota(jnp.int32, (256, K), 0) + at
        p1[at : at + 256, :] = jnp.where(index == sk1, 1.0, 0.0).astype(BF)
        p2[at : at + 256, :] = jnp.where(index == sk2, 1.0, 0.0).astype(BF)
    skt[...] = jnp.transpose(jnp.broadcast_to(sk1.astype(F32), (128, K)))

    pl.semaphore_wait(barrier, len(peers))

    t_if = remote(leaf.at[1 - c, 0, 0, 1 - c], ifc.at[c], ssem.at[0], rsem.at[0], sib)
    t_w1 = remote(w1.at[:, 0], wa.at[:, w1_rows, :], ssem.at[1], rsem.at[1], sib)
    t_w2 = remote(w2.at[:, 0], wb.at[:, w2_rows, :], ssem.at[2], rsem.at[2], sib)
    t_w2i = remote(w2.at[0, 0], wb.at[0, w2_rows, :], ssem.at[3], rsem.at[3], inner)
    t_w2o = remote(w2.at[1, 0], wb.at[1, w2_rows, :], ssem.at[4], rsem.at[4], outer)
    q2 = pl.ds(pl.multiple_of((q + 2 - 4 * h) * (K // 4), 16), K // 4)
    t_w2fi = remote(wb.at[0, q2, :], wb.at[0, q2, :], ssem.at[5], rsem.at[5], sib)
    t_w2fo = remote(wb.at[1, q2, :], wb.at[1, q2, :], ssem.at[6], rsem.at[6], sib)
    own_xs = pl.ds(pl.multiple_of(c * K, 16), K)
    t_xs = remote(xs.at[own_xs, :], xs.at[own_xs, :], ssem.at[7], rsem.at[7], sib)
    t_pick = remote(stg.at[1 - h], pex, ssem.at[8], rsem.at[8], (cross_box, f))
    first_a = {
        d: remote(chunk_of(f ^ d), xs.at[own_rows, :], asend.at[d - 1], arecv.at[d - 1], (b, f ^ d)) for d in range(1, 8)
    }

    def part_rows(face, rows, cols):
        at, n = rows
        return ga.at[pl.ds(pl.multiple_of(c * K + face * fr + at, 16), n), cols[0] : cols[0] + cols[1]]

    def plane_rows(node, rows, cols):
        at, n = rows
        return gt.at[node[0], :, pl.ds(pl.multiple_of(node[1] * fr + at, 16), n), cols[0] : cols[0] + cols[1]]

    ag1 = face_gather(part_rows, (s1, r1, ds1, dr1), b, f, sib, fr)
    ag2 = plane_gather(plane_rows, (s2, r2s, ds2, dr2), b, f, h, cross_box, sib, fr)

    t_if.start()
    for d in EARLY:
        first_a[d].start()
    t_w1.start()
    t_w2.start()

    loc_if.wait()
    t_if.wait_recv()
    ga[own_rows, 0:K] = ifc[0, :, 0:K]
    ga[own_rows, K : 2 * K] = ifc[1, :, K : 2 * K]
    ga[own_rows, 2 * K :] = (
        fdot(ifc[0, :, 2 * K :], p1[0:K, :]) + fdot(ifc[1, :, 2 * K :], p1[K:, :])
    ).astype(BF)
    ag1.go(0, 1, 2, 3, 4, 5)
    ag1.hand(0)

    def coupled(rows, side, left, left2, weights, pick, dest):
        couple = rows[:, :, pl.ds(pl.multiple_of((1 - side) * K, 128), K)]
        write_left(left, couple[0], couple[1])
        hid = fdot(left[...], weights[...].reshape(2 * K, K)).astype(BF)
        write_left(left2, hid[:fr], hid[fr:])
        side_cols = rows[:, :, 2 * K :].reshape(2 * fr, K)
        half = pick[pl.ds(pl.multiple_of(side * K, 16), K), :]
        dest[...] = fdot(side_cols, half).astype(BF)

    def base_of(rows, side, dest, block):
        if block == 2:
            return dest[...].astype(F32)
        on = jnp.where(side == block, 1.0, 0.0)
        return rows[:, :, block * K : (block + 1) * K].reshape(2 * fr, K).astype(F32) * on

    loc_end.wait()
    loc_w1.wait()
    t_w1.wait_recv()
    coupled(endr, c, lh, lh2, wa, p1, dp)

    ag1.got(1)
    ag1.go(6, 8)
    ag1.got(2)
    ag1.go(7, 9)
    ag1.got(0)
    ag1.go(10, 11)
    ag1.hand(1)
    ag1.got(3)
    ag1.hand(2)
    ag1.got(4)
    ag1.hand(3)
    ag1.go(14, 15)
    ag1.got(6)
    ag1.go(12)
    ag1.got(7)
    ag1.go(13)
    ag1.hand(4)
    for d in range(1, 8):
        if d not in EARLY:
            first_a[d].start()
    ag1.got(5)
    ag1.hand(6)
    ag1.got(8)
    ag1.hand(9)
    ag1.got(9)
    ag1.hand(10)
    ag1.got(10)
    ag1.go(16)
    ag1.hand(7)
    ag1.got(11)
    ag1.go(17)
    ag1.hand(8)
    t_w2i.start()
    t_w2o.start()
    ag1.got(14, 15)
    ag1.hand(5)
    ag1.got(12, 13)
    ag1.hand(11)
    loc_xs.wait()
    for copy in first_a.values():
        copy.wait_recv()
    t_xs.start()
    ag1.got(16, 17)
    ag1.hand(12)
    ag1.handed()

    @pl.when(mid)
    def _():
        sides = (base_of(endr, c, dp, 2) - fdot(lh2[...], ga[:, 2 * K :])).astype(BF)
        half = p2[pl.ds(pl.multiple_of(h * K, 16), K), :]
        stg[...] = fdot(sides, half).astype(BF).reshape(2, fr, K)
        t_pick.start()
        ends = fdot(lh2[...], ga[:, pl.ds(pl.multiple_of(h * K, 128), K)])
        gt[h, 0:2, face_rows, :] = (-ends).astype(BF).reshape(2, fr, K)

    @pl.when(jnp.logical_not(mid))
    def _():
        for block in (2, 0, 1):
            cols = slice(block * K, (block + 1) * K)
            value = base_of(endr, c, dp, block) - fdot(lh2[...], ga[:, cols])
            r2[:, :, cols] = value.astype(BF).reshape(2, fr, K)

    t_xs.wait_recv()
    lane = lax.broadcasted_iota(jnp.int32, (256, 128), 1)
    mine = skt[pl.ds(pl.multiple_of(c * 256, 16), 256), :].astype(jnp.int32)
    total = None
    for part in range(8):
        hot = jnp.where(mine == lane + part * 128, 1.0, 0.0).astype(BF)
        term = fdot(hot, xs[part * 128 : (part + 1) * 128, :])
        total = term if total is None else total + term
    sel[...] = total.astype(BF)
    into = srow.at[f // 4, :, pl.ds(pl.multiple_of(lw * (f % 4), 128), lw)]
    dest_box = b - c + 1 - h
    here = jnp.logical_and(f // 4 == c, mid)

    def back(i):
        turn = (f + i) % 4
        src = sel.at[pl.ds(pl.multiple_of(turn * fr, 16), fr), :]
        return src, remote(src, into, bsend.at[i], brecv.at[f], (dest_box, 4 * c + turn))

    for i in (2, 1, 3):
        back(i)[1].start()

    @pl.when(here)
    def _():
        pltpu.make_async_copy(back(0)[0], into, brecv.at[f]).start()

    @pl.when(jnp.logical_not(here))
    def _():
        back(0)[1].start()

    @pl.when(mid)
    def _():
        t_pick.wait_recv()
        gt[h, 2, face_rows, :] = stg[h] + pex[...]
        ag2.go(0, 1, 4, 5, 24, 25, 8, 9)
        ag2.hand(0)

        for j in range(8):
            view = srow.at[j // 4, :, lw * (j % 4) : lw * (j % 4 + 1)]
            pltpu.make_async_copy(view, view, brecv.at[j]).wait()
        seen = skt[face_rows, :]
        left1 = jnp.tile(jnp.where(seen < K, 1.0, 0.0), (1, 4)).astype(BF)
        right1 = 1 - left1
        left = jnp.concatenate([left1, left1], axis=0)
        right = 1 - left
        couple = [srow[t, :, K : 2 * K] * left1 + srow[t, :, 0:K] * right1 for t in range(2)]
        write_left(lhs_s, couple[0], couple[1])
        hid = fdot(lhs_s[...], wa[...].reshape(2 * K, K)).astype(BF)
        write_left(lh2_s, hid[:fr], hid[fr:])
        sides = srow[:, :, 2 * K :].reshape(2 * fr, K)
        dps[...] = (fdot(sides * left, p1[0:K, :]) + fdot(sides * right, p1[K:, :])).astype(BF)
        for block in (2, 0, 1):
            prod = fdot(lh2_s[...], ga[:, block * K : (block + 1) * K])
            if block == 2:
                base = dps[...].astype(F32)
            else:
                on = left if block == 0 else right
                base = (srow[:, :, block * K : (block + 1) * K].reshape(2 * fr, K) * on).astype(F32)
            r2[:, :, block * K : (block + 1) * K] = (base - prod).astype(BF).reshape(2, fr, K)

        ag2.got(0)
        ag2.go(2)
        ag2.got(1)
        ag2.go(3)
        ag2.got(4)
        ag2.go(6)
        ag2.got(5)
        ag2.go(7)
        ag2.go(12, 13, 28, 29, 16, 17, 32, 33)

    t_w2i.wait_recv()
    t_w2fi.start()
    t_w2o.wait_recv()
    t_w2fo.start()

    @pl.when(mid)
    def _():
        ag2.got(24, 25)
        ag2.go(26, 27)
        ag2.got(8, 9)
        ag2.go(10, 11)
        ag2.got(2, 3)
        ag2.go(20, 21)
        ag2.got(6, 7)
        ag2.go(36, 37)

    loc_w2.wait()
    t_w2.wait_recv()
    t_w2fi.wait_recv()
    t_w2fo.wait_recv()
    coupled(r2, h, lh, lh2, wb, p2, dp)

    @pl.when(mid)
    def _():
        for i in (1, 2, 3):
            ag2.got(8 + 4 * i)
            ag2.go(10 + 4 * i)
            ag2.got(9 + 4 * i)
            ag2.go(11 + 4 * i)
            ag2.got(24 + 4 * i)
            ag2.go(26 + 4 * i)
            ag2.got(25 + 4 * i)
            ag2.go(27 + 4 * i)
            if i == 1:
                ag2.hand(1, 2, 4, 8)
                ag2.got(26, 27)
                ag2.hand(3)
                ag2.got(10, 11)
                ag2.hand(12)
            if i == 2:
                ag2.hand(5, 6, 9, 10)
        for i in (1, 2):
            ag2.got(10 + 4 * i, 11 + 4 * i)
            ag2.got(26 + 4 * i, 27 + 4 * i)
        ag2.hand(13, 14, 7, 11)
        ag2.got(22, 23)
        ag2.got(38, 39)
        ag2.hand(15)

    @pl.when(jnp.logical_not(mid))
    def _():
        ag2.handed()

    left = lh2[...]
    for block in (0, 1, 2):
        cols = slice(block * K, (block + 1) * K)
        if block == 2:
            prod = fdot(left[:, :K], gt[0, 2]) + fdot(left[:, K:], gt[1, 2])
        else:
            prod = fdot(left, gt[block, 0:2].reshape(2 * K, K))
        value = base_of(r2, h, dp, block) - prod
        res[:, 0, :, cols] = value.astype(BF).reshape(2, fr, K)
        view = (slice(None), slice(None), slice(None), cols)
        local(7 + block, res.at[view], out.at[view])

    for copy in [t_if, t_w1, t_w2, t_w2i, t_w2o, t_w2fi, t_w2fo, t_xs] + list(first_a.values()):
        copy.wait_send()
    for i in (1, 2, 3):
        back(i)[1].wait_send()

    @pl.when(jnp.logical_not(here))
    def _():
        back(0)[1].wait_send()

    ag1.drain()

    @pl.when(mid)
    def _():
        t_pick.wait_send()
        ag2.drain()

    for block in range(3):
        view = (slice(None), slice(None), slice(None), slice(block * K, (block + 1) * K))
        pltpu.make_async_copy(res.at[view], out.at[view], lsem.at[7 + block]).wait()


def on_device(leaf, w1, w2, skel1, skel2):
    fr = leaf.shape[4]
    any_spec = pl.BlockSpec(memory_space=pl.ANY)
    dma = pltpu.SemaphoreType.DMA
    lw = 3 * 2 * K // 8
    scratch = [
        pltpu.VMEM(skel1.shape, jnp.int32),
        pltpu.VMEM(skel2.shape, jnp.int32),
        pltpu.VMEM((2, fr, 3 * K), BF),
        pltpu.VMEM((2, fr, 3 * K), BF),
        pltpu.VMEM((2 * K, lw), BF),
        pltpu.VMEM((K // 2, lw), BF),
        pltpu.VMEM((2, fr, 3 * K), BF),
        pltpu.VMEM((2 * K, K), BF),
        pltpu.VMEM((2 * K, K), BF),
        pltpu.VMEM((K, 128), F32),
        pltpu.VMEM((2, K, K), BF),
        pltpu.VMEM((2, K, K), BF),
        pltpu.VMEM((2 * K, 3 * K), BF),
        pltpu.VMEM((2, 3, K, K), BF),
        pltpu.VMEM((2 * fr, 2 * K), BF),
        pltpu.VMEM((2 * fr, 2 * K), BF),
        pltpu.VMEM((2 * fr, 2 * K), BF),
        pltpu.VMEM((2 * fr, 2 * K), BF),
        pltpu.VMEM((2 * fr, K), BF),
        pltpu.VMEM((2 * fr, K), BF),
        pltpu.VMEM((2, fr, 3 * K), BF),
        pltpu.VMEM((2, fr, K), BF),
        pltpu.VMEM((fr, K), BF),
        pltpu.VMEM((2, 1, fr, 3 * K), BF),
        dma((10,)),
        dma((9,)),
        dma((9,)),
        dma((18,)),
        dma((18,)),
        dma((13,)),
        dma((13,)),
        dma((40,)),
        dma((40,)),
        dma((16,)),
        dma((16,)),
        dma((7,)),
        dma((7,)),
        dma((4,)),
        dma((8,)),
    ]
    return pl.pallas_call(
        functools.partial(kernel, fr),
        out_shape=jax.ShapeDtypeStruct((2, 1, fr, 3 * K), BF),
        in_specs=[any_spec] * 5,
        out_specs=any_spec,
        scratch_shapes=scratch,
        compiler_params=pltpu.CompilerParams(
            collective_id=0, has_side_effects=True, vmem_limit_bytes=67043328
        ),
    )(leaf, w1, w2, skel1, skel2)


def solution(mesh):
    return jax.shard_map(
        on_device,
        mesh=mesh,
        in_specs=(
            P(None, None, "box", None, "face", None),
            P(None, None, "box", None),
            P(None, None, "box", None),
            P(),
            P(),
        ),
        out_specs=P(None, None, ("box", "face"), None),
        check_vma=False,
    )
```

time: 58.6 us -> 51.7 us (0.88)
  local copies, waits for them, and re-layouts: 5.48 us -> 1.77 us
  Pallas kernels: 52.8 us -> 49.6 us
    unnamed x11 -> x1, local copies, waits for them, and re-layouts: 5.48 us -> 1.77 us
    pallas_call x1, Pallas kernels: 52.8 us -> 49.6 us  [on_device(): pl.pallas_call(functools.partial(kernel, fr), out_shape=jax.ShapeDtypeStr...]
where the time goes in v2:
time: 51.7 us; the launch traced here: 51.4 us
  Pallas kernels  49.6 us (96%)
  local copies, waits for them, and re-layouts  1.77 us (3%)
    pallas_call x1, Pallas kernels, on_device(): pl.pallas_call(functools.partial(kernel, fr), out_shape=jax.ShapeDtypeStr...  49.6 us
    unnamed x1, local copies, waits for them, and re-layouts  1.77 us

profile of v2, /device:TPU:1, one launch (start us, length us, event | category | flops | bytes accessed | tf_op | source)
XLA Modules:
  0.0 51.4 jit_solution(13217290661959969446)
XLA Ops:
  0.0 49.6 %shard_map.55 = bf16[2,1,64,1536]{3,2,1,0:T(8,128)(2,1)} custom-call(bf16[2,1,1,3,64,1536]{5,4,3,2,1,0:T(8,128)(2,1)} %leaf.1, bf16[2,1,256,512]{3,2,1,0:T(8,128)(2,1)} %w1.1, bf16[2,1,128,512]{3,2,1,0:T(8,128)(2,1)} %w2.1, s32[1,16,512]{2,1,0:T(8,128)} %skel1.1, s32[1,8,512]{2,1,0:T(8,128)} %skel2.1), custom_call_target="tpu_custom_call" | custom-call | tf_op jit(solution)/shard_map/pallas_call | solution.py:549
  49.6 1.8 %copy.7 = bf16[2,1,64,1536]{3,2,1,0:T(8,128)(2,1)} copy(bf16[2,1,64,1536]{3,2,1,0:T(8,128)(2,1)} %shard_map.55) | data formatting | bytes 786432

commit v3 on v2

v3 whole, which is shorter than its diff:
```python
import functools

import jax
import jax.numpy as jnp
from jax import lax
from jax.experimental import pallas as pl
from jax.experimental.pallas import tpu as pltpu
from jax.sharding import PartitionSpec as P

K = 512
BF = jnp.bfloat16
F32 = jnp.float32
MESH = pl.DeviceIdType.MESH
GRANT = 48 * 1024 * 1024


def fdot(a, b):
    return jnp.dot(a, b, preferred_element_type=F32)


def remote(src, dst, send, recv, target):
    return pltpu.make_async_remote_copy(
        src_ref=src, dst_ref=dst, send_sem=send, recv_sem=recv, device_id=target, device_id_type=MESH
    )


def write_left(ref, real, imag):
    n = real.shape[0]
    ref[0:n, 0:K] = real
    ref[0:n, K : 2 * K] = -imag
    ref[n : 2 * n, 0:K] = imag
    ref[n : 2 * n, K : 2 * K] = real


class Gather:
    def __init__(self, view, send, recv, dsend, drecv, sib):
        self.view, self.send, self.recv, self.dsend, self.drecv, self.sib = view, send, recv, dsend, drecv, sib
        self.hops, self.hands = [], []

    def hop(self, k):
        what, to = self.hops[k]
        ref = self.view(*what)
        return remote(ref, ref, self.send.at[0], self.recv.at[k], to)

    def hand_over(self, k):
        ref = self.view(*self.hands[k])
        return remote(ref, ref, self.dsend.at[0], self.drecv.at[0], self.sib)

    def got(self, *ks):
        for k in ks:
            self.hop(k).wait_recv()

    def go(self, *ks):
        for k in ks:
            self.hop(k).start()

    def hand(self, *ks):
        for k in ks:
            self.hand_over(k).start()


def settle(view, sem):
    pltpu.make_async_copy(view, view, sem).wait()


def face_gather(view, sems, b, f, c, sib):
    g = Gather(view, *sems, sib)
    y, xh = f // 2, f % 2

    def at(dy, dx):
        return (c, ((y + dy) % 4) * 2 + (xh + dx) % 2)

    own, up, down, far = at(0, 0), at(1, 0), at(3, 0), at(2, 0)
    side, up_side, down_side, far_side = at(0, 1), at(1, 1), at(3, 1), at(2, 1)
    lo, hi, full = (0, K // 2), (K // 2, K // 2), (0, K)
    x, u, d = (b, side[1]), (b, up[1]), (b, down[1])
    for piece in ((0, 1), (2, 1)):
        g.hops += [
            ((own, piece, full), x),
            ((own, piece, full), u),
            ((own, piece, full), d),
            ((side, piece, full), u),
            ((side, piece, full), d),
            ((down, piece, lo), u),
            ((up, piece, hi), d),
            ((down_side, piece, lo), u),
            ((up_side, piece, hi), d),
        ]
    piece = (1, 1)
    g.hops += [
        ((own, piece, full), u),
        ((own, piece, full), d),
        ((own, piece, full), x),
        ((down, piece, lo), u),
        ((up, piece, hi), d),
        ((down, piece, full), x),
        ((up, piece, full), x),
        ((far, piece, lo), x),
        ((far, piece, hi), x),
    ]
    ends, picked, every = (0, 2), (2, 1), (0, 3)
    g.hands = [
        (own, every, full),
        (side, ends, full),
        (down, every, full),
        (up, every, full),
        (side, picked, full),
        (down_side, every, full),
        (up_side, every, full),
        (far, every, full),
        (far_side, ends, full),
        (far_side, picked, full),
    ]
    return g


def plane_gather(view, sems, b, f, h, cross_box, sib, fr):
    g = Gather(view, *sems, sib)
    y, xh = f // 2, f % 2

    def face(dy, dx):
        return ((y + dy) % 4) * 2 + (xh + dx) % 2

    xs = [(h, 0), (1 - h, 0), (1 - h, 1), (h, 1)]
    ys = [0, 1, 3, 2]

    def node(iy, ix):
        return (xs[ix][0], face(ys[iy], xs[ix][1]))

    alpha, beta = (0, fr // 2), (fr // 2, fr // 2)
    lo, hi, full = (0, K // 2), (K // 2, K // 2), (0, K)
    inner, outer = (cross_box, f), (cross_box, face(0, 1))
    up, down = (b, face(1, 0)), (b, face(3, 0))
    g.hops += [
        ((node(0, 0), alpha, full), inner),
        ((node(0, 0), alpha, full), outer),
        ((node(0, 1), alpha, lo), outer),
        ((node(0, 2), alpha, hi), inner),
    ]
    g.hops += [
        ((node(0, 0), beta, full), up),
        ((node(0, 0), beta, full), down),
        ((node(2, 0), beta, lo), up),
        ((node(1, 0), beta, hi), down),
    ]
    for i in range(4):
        g.hops += [
            ((node(0, i), alpha, full), up),
            ((node(0, i), alpha, full), down),
            ((node(2, i), alpha, lo), up),
            ((node(1, i), alpha, hi), down),
        ]
    for i in range(4):
        g.hops += [
            ((node(i, 0), beta, full), inner),
            ((node(i, 0), beta, full), outer),
            ((node(i, 1), beta, lo), outer),
            ((node(i, 2), beta, hi), inner),
        ]
    g.hands = [(node(i // 2 // 4, i // 2 % 4), (alpha, beta)[i % 2], full) for i in range(32)]
    return g


def kernel(fr, leaf, w1, w2, skel1, skel2, out, sk1v, sk2v, ifs, endr, xs, sel, srow, p1, p2, skt, wa, wb, ga, gt,
           lh, lh2, lhs_s, lh2_s, dp, dps, r2, stg, pex, lsem, ssem, rsem, s1, r1, ds1, dr1, s2, r2s, ds2, dr2,
           asend, arecv, bsend, brecv):
    b, f = lax.axis_index("box"), lax.axis_index("face")
    c, h = b % 2, (b // 2) % 2
    q = b % 4
    sib = (b + 1 - 2 * c, f)
    inner_box = b + 2 - 4 * h
    other_face = f // 2 * 2 + 1 - f % 2
    inner, outer = (inner_box, f), (inner_box, other_face)
    cross_box = inner_box + 1 - 2 * c
    mid = c != h
    not_mid = jnp.logical_not(mid)

    barrier = pltpu.get_barrier_semaphore()
    peers = [(b, f ^ d) for d in range(1, 8)] + [(sib[0], f ^ d) for d in range(8)]
    peers += [inner, outer, (cross_box, f), (cross_box, other_face)]
    for peer in peers:
        pl.semaphore_signal(barrier, inc=1, device_id=peer, device_id_type=MESH)

    def local(k, src, dst):
        copy = pltpu.make_async_copy(src, dst, lsem.at[k])
        copy.start()
        return copy

    loc_s1 = local(5, skel1, sk1v)
    loc_s2 = local(6, skel2, sk2v)
    lw = 3 * 2 * K // 8
    face_rows = pl.ds(pl.multiple_of(f * fr, 16), fr)
    own_rows = pl.ds(pl.multiple_of(c * K + f * fr, 16), fr)
    own_cols = pl.ds(pl.multiple_of(c * K, 128), K)
    loc_ga = local(7, leaf.at[:, 0, 0, 1 - c, :, own_cols], ga.at[c, 0:2, face_rows, :])
    loc_if = local(0, leaf.at[c, 0, 0, 1 - c, :, 2 * K : 3 * K], ifs.at[c])
    loc_end = local(1, leaf.at[:, 0, 0, c], endr)

    def chunk_of(j):
        return leaf.at[j // 4, 0, 0, 2, :, pl.ds(pl.multiple_of(lw * (j % 4), 128), lw)]


    @pl.when(not_mid)
    def _():
        pltpu.make_async_copy(chunk_of(f), xs.at[own_rows, :], lsem.at[2]).start()

    w1_rows = pl.ds(pl.multiple_of(c * (K // 2), 16), K // 2)
    w2_rows = pl.ds(pl.multiple_of(q * (K // 4), 16), K // 4)
    loc_w1 = local(3, w1.at[:, 0], wa.at[:, w1_rows, :])
    loc_w2 = local(4, w2.at[:, 0], wb.at[:, w2_rows, :])

    loc_s1.wait()
    loc_s2.wait()
    sk1 = sk1v[0, pl.ds(b // 2, 1), :]
    sk2 = sk2v[0, pl.ds(b // 4, 1), :]
    for part in range(4):
        at = part * 256
        index = lax.broadcasted_iota(jnp.int32, (256, K), 0) + at
        p1[at : at + 256, :] = jnp.where(index == sk1, 1.0, 0.0).astype(BF)
        p2[at : at + 256, :] = jnp.where(index == sk2, 1.0, 0.0).astype(BF)
    skt[...] = jnp.transpose(jnp.broadcast_to(sk1.astype(F32), (128, K)))
    loc_ga.wait()

    pl.semaphore_wait(barrier, len(peers))

    t_if = remote(leaf.at[1 - c, 0, 0, 1 - c, :, 2 * K : 3 * K], ifs.at[c], ssem.at[0], rsem.at[0], sib)
    t_w1 = remote(w1.at[:, 0], wa.at[:, w1_rows, :], ssem.at[1], rsem.at[1], sib)
    t_w2 = remote(w2.at[:, 0], wb.at[:, w2_rows, :], ssem.at[2], rsem.at[2], sib)
    t_w2i = remote(w2.at[0, 0], wb.at[0, w2_rows, :], ssem.at[3], rsem.at[3], inner)
    t_w2o = remote(w2.at[1, 0], wb.at[1, w2_rows, :], ssem.at[4], rsem.at[4], outer)
    q2 = pl.ds(pl.multiple_of((q + 2 - 4 * h) * (K // 4), 16), K // 4)
    t_w2fi = remote(wb.at[0, q2, :], wb.at[0, q2, :], ssem.at[5], rsem.at[5], sib)
    t_w2fo = remote(wb.at[1, q2, :], wb.at[1, q2, :], ssem.at[6], rsem.at[6], sib)
    t_xs = remote(chunk_of(f), xs.at[own_rows, :], ssem.at[7], rsem.at[7], sib)
    t_pick = remote(stg.at[1 - h], pex, ssem.at[8], rsem.at[8], (cross_box, f))
    picker_box = b - c + h

    def spread_side():
        for d in (7, 5, 3, 1, 6, 4, 2):
            remote(chunk_of(f ^ d), xs.at[own_rows, :], asend.at[0], arecv.at[0], (picker_box, f ^ d)).start()


    def part_rows(node, blocks, cols):
        rows = pl.ds(pl.multiple_of(node[1] * fr, 16), fr)
        return ga.at[node[0], blocks[0] : blocks[0] + blocks[1], rows, cols[0] : cols[0] + cols[1]]

    def plane_rows(node, rows, cols):
        at, n = rows
        return gt.at[node[0], :, pl.ds(pl.multiple_of(node[1] * fr + at, 16), n), cols[0] : cols[0] + cols[1]]

    ag1 = face_gather(part_rows, (s1, r1, ds1, dr1), b, f, c, sib)
    ag2 = plane_gather(plane_rows, (s2, r2s, ds2, dr2), b, f, h, cross_box, sib, fr)

    t_if.start()
    ag1.go(18, 19, 0, 1, 2, 20)
    t_w1.start()
    t_w2.start()

    loc_if.wait()
    t_if.wait_recv()
    ga[c, 2, face_rows, :] = (fdot(ifs[0], p1[0:K, :]) + fdot(ifs[1], p1[K:, :])).astype(BF)
    ag1.go(9, 10, 11)
    ag1.hand(0)

    def coupled(rows, side, left, left2, weights, pick, dest):
        couple = rows[:, :, pl.ds(pl.multiple_of((1 - side) * K, 128), K)]
        write_left(left, couple[0], couple[1])
        hid = fdot(left[...], weights[...].reshape(2 * K, K)).astype(BF)
        write_left(left2, hid[:fr], hid[fr:])
        side_cols = rows[:, :, 2 * K :].reshape(2 * fr, K)
        half = pick[pl.ds(pl.multiple_of(side * K, 16), K), :]
        dest[...] = fdot(side_cols, half).astype(BF)

    def base_of(rows, side, dest, block):
        if block == 2:
            return dest[...].astype(F32)
        on = jnp.where(side == block, 1.0, 0.0)
        return rows[:, :, block * K : (block + 1) * K].reshape(2 * fr, K).astype(F32) * on

    def times(left2, gathered, block):
        if block == 2:
            left = left2[...]
            return fdot(left[:, :K], gathered[0, 2]) + fdot(left[:, K:], gathered[1, 2])
        return fdot(left2[...], gathered[block, 0:2].reshape(2 * K, K))

    loc_end.wait()
    loc_w1.wait()
    t_w1.wait_recv()
    coupled(endr, c, lh, lh2, wa, p1, dp)

    ag1.got(18)
    ag1.go(21, 23)
    ag1.got(19)
    ag1.go(22, 24)
    ag1.got(0)
    ag1.go(3, 4)
    ag1.got(1)
    ag1.go(5)
    ag1.got(2)
    ag1.go(6)
    ag1.got(20)
    ag1.hand(1)
    ag1.got(21)
    ag1.go(25)
    ag1.got(22)
    ag1.go(26)
    t_w2i.start()
    t_w2o.start()
    ag1.got(9)
    ag1.go(12, 13)
    ag1.hand(4)
    ag1.got(10)
    ag1.go(14)
    ag1.hand(2)
    ag1.got(11)
    ag1.go(15)
    ag1.hand(3)
    ag1.got(3)
    ag1.go(7)
    ag1.got(4)
    ag1.go(8)
    ag1.got(12)
    ag1.go(16)
    ag1.got(13)
    ag1.go(17)

    @pl.when(mid)
    def _():
        t_xs.start()
        spread_side()

    ag1.got(23)
    ag1.hand(5)
    ag1.got(24)
    ag1.hand(6)
    ag1.got(5, 6, 14, 15)
    ag1.hand(7)
    ag1.got(25, 26, 7, 8)
    ag1.hand(8)
    ag1.got(16, 17)
    ag1.hand(9)

    @pl.when(not_mid)
    def _():
        spread_side()

    settle(ga.at[0], dr1.at[0])

    into = srow.at[f // 4, :, pl.ds(pl.multiple_of(lw * (f % 4), 128), lw)]
    dest_box = b - c + 1 - h

    def pass_w2():
        t_w2i.wait_recv()
        t_w2fi.start()
        t_w2o.wait_recv()
        t_w2fo.start()

    def side_select():
        pltpu.make_async_copy(chunk_of(f), xs.at[own_rows, :], lsem.at[2]).wait()
        t_xs.wait_recv()
        settle(xs.at[0 : 14 * fr, :], arecv.at[0])
        lane = lax.broadcasted_iota(jnp.int32, (K, 128), 1)
        mine = skt[...].astype(jnp.int32)
        total = None
        for part in range(8):
            hot = jnp.where(mine == lane + part * 128, 1.0, 0.0).astype(BF)
            term = fdot(hot, xs[part * 128 : (part + 1) * 128, :])
            total = term if total is None else total + term
        sel[...] = total.astype(BF)
        for d in (7, 5, 3, 1, 6, 4, 2, 0):
            rows = pl.ds(pl.multiple_of((f ^ d) * fr, 16), fr)
            remote(sel.at[rows, :], into, bsend.at[0], brecv.at[0], (dest_box, f ^ d)).start()

    def level_two():
        loc_w2.wait()
        t_w2.wait_recv()
        t_w2fi.wait_recv()
        t_w2fo.wait_recv()
        coupled(r2, h, lh, lh2, wb, p2, dp)

    def third(i):
        ag2.got(8 + 4 * i)
        ag2.go(10 + 4 * i)
        ag2.hand(2 * (8 + i))
        ag2.got(9 + 4 * i)
        ag2.go(11 + 4 * i)
        ag2.hand(2 * (4 + i))
        ag2.got(24 + 4 * i)
        ag2.go(26 + 4 * i)
        ag2.hand(2 * (4 * i + 1) + 1)
        ag2.got(25 + 4 * i)
        ag2.go(27 + 4 * i)
        ag2.hand(2 * (4 * i + 2) + 1)

    @pl.when(mid)
    def _():
        sides = (base_of(endr, c, dp, 2) - times(lh2, ga, 2)).astype(BF)
        half = p2[pl.ds(pl.multiple_of(h * K, 16), K), :]
        stg[...] = fdot(sides, half).astype(BF).reshape(2, fr, K)
        t_pick.start()
        ends = fdot(lh2[...], ga[h, 0:2].reshape(2 * K, K))
        gt[h, 0:2, face_rows, :] = (-ends).astype(BF).reshape(2, fr, K)
        pass_w2()
        t_pick.wait_recv()
        gt[h, 2, face_rows, :] = stg[h] + pex[...]
        ag2.go(0, 1, 4, 5, 24, 25, 8, 9)
        ag2.hand(0, 1)
        ag2.got(0)
        ag2.go(2)
        ag2.got(1)
        ag2.go(3)
        ag2.got(4)
        ag2.go(6)
        ag2.got(5)
        ag2.go(7)
        ag2.go(12, 13, 28, 29, 16, 17, 32, 33)
        ag2.hand(2, 4, 9, 17)
        ag2.got(24, 25)
        ag2.go(26, 27)
        ag2.got(8, 9)
        ag2.go(10, 11)
        ag2.hand(3, 5, 8, 16)
        ag2.got(2, 3)
        ag2.go(20, 21)
        ag2.got(6, 7)
        ag2.go(36, 37)
        ag2.hand(6, 25)
        third(1)
        ag2.got(26, 27)
        ag2.got(10, 11)
        ag2.hand(7, 24)

        settle(srow, brecv.at[0])
        seen = skt[face_rows, :]
        left1 = jnp.tile(jnp.where(seen < K, 1.0, 0.0), (1, 4)).astype(BF)
        right1 = 1 - left1
        left = jnp.concatenate([left1, left1], axis=0)
        right = 1 - left
        couple = [srow[t, :, K : 2 * K] * left1 + srow[t, :, 0:K] * right1 for t in range(2)]
        write_left(lhs_s, couple[0], couple[1])
        hid = fdot(lhs_s[...], wa[...].reshape(2 * K, K)).astype(BF)
        write_left(lh2_s, hid[:fr], hid[fr:])
        sides = srow[:, :, 2 * K :].reshape(2 * fr, K)
        dps[...] = (fdot(sides * left, p1[0:K, :]) + fdot(sides * right, p1[K:, :])).astype(BF)
        for block in (2, 0, 1):
            if block == 2:
                base = dps[...].astype(F32)
            else:
                on = left if block == 0 else right
                base = (srow[:, :, block * K : (block + 1) * K].reshape(2 * fr, K) * on).astype(F32)
            value = base - times(lh2_s, ga, block)
            r2[:, :, block * K : (block + 1) * K] = value.astype(BF).reshape(2, fr, K)

        third(2)
        level_two()
        third(3)
        for i in (1, 2):
            ag2.got(10 + 4 * i, 11 + 4 * i)
            ag2.hand(2 * (12 + i))
            ag2.got(26 + 4 * i, 27 + 4 * i)
            ag2.hand(2 * (4 * i + 3) + 1)
        ag2.got(22, 23)
        ag2.hand(30)
        ag2.got(38, 39)
        ag2.hand(31)

    @pl.when(not_mid)
    def _():
        for block in (2, 0, 1):
            value = base_of(endr, c, dp, block) - times(lh2, ga, block)
            r2[:, :, block * K : (block + 1) * K] = value.astype(BF).reshape(2, fr, K)
        pass_w2()
        side_select()
        level_two()
        settle(gt, dr2.at[0])

    for block in (0, 1, 2):
        value = base_of(r2, h, dp, block) - times(lh2, gt, block)
        out[:, 0, :, block * K : (block + 1) * K] = value.astype(BF).reshape(2, fr, K)

    for copy in [t_if, t_w1, t_w2, t_w2i, t_w2o, t_w2fi, t_w2fo]:
        copy.wait_send()
    settle(xs.at[0 : 7 * fr, :], asend.at[0])
    settle(ga.at[0, :, 0 : 7 * fr, :], s1.at[0])
    settle(ga.at[0], ds1.at[0])

    @pl.when(mid)
    def _():
        t_xs.wait_send()
        t_pick.wait_send()
        settle(gt.at[:, :, 0 : K - fr // 2, :], s2.at[0])
        settle(gt, ds2.at[0])

    @pl.when(not_mid)
    def _():
        settle(sel, bsend.at[0])


def on_device(leaf, w1, w2, skel1, skel2):
    fr = leaf.shape[4]
    hbm_spec = pl.BlockSpec(memory_space=pltpu.HBM)
    dma = pltpu.SemaphoreType.DMA
    lw = 3 * 2 * K // 8
    scratch = [
        pltpu.VMEM(skel1.shape, jnp.int32),
        pltpu.VMEM(skel2.shape, jnp.int32),
        pltpu.VMEM((2, fr, K), BF),
        pltpu.VMEM((2, fr, 3 * K), BF),
        pltpu.VMEM((2 * K, lw), BF),
        pltpu.VMEM((K, lw), BF),
        pltpu.VMEM((2, fr, 3 * K), BF),
        pltpu.VMEM((2 * K, K), BF),
        pltpu.VMEM((2 * K, K), BF),
        pltpu.VMEM((K, 128), F32),
        pltpu.VMEM((2, K, K), BF),
        pltpu.VMEM((2, K, K), BF),
        pltpu.VMEM((2, 3, K, K), BF),
        pltpu.VMEM((2, 3, K, K), BF),
        pltpu.VMEM((2 * fr, 2 * K), BF),
        pltpu.VMEM((2 * fr, 2 * K), BF),
        pltpu.VMEM((2 * fr, 2 * K), BF),
        pltpu.VMEM((2 * fr, 2 * K), BF),
        pltpu.VMEM((2 * fr, K), BF),
        pltpu.VMEM((2 * fr, K), BF),
        pltpu.VMEM((2, fr, 3 * K), BF),
        pltpu.VMEM((2, fr, K), BF),
        pltpu.VMEM((fr, K), BF),
        dma((8,)),
        dma((9,)),
        dma((9,)),
        dma((1,)),
        dma((27,)),
        dma((1,)),
        dma((1,)),
        dma((1,)),
        dma((40,)),
        dma((1,)),
        dma((1,)),
        dma((1,)),
        dma((1,)),
        dma((1,)),
        dma((1,)),
    ]
    return pl.pallas_call(
        functools.partial(kernel, fr),
        out_shape=jax.ShapeDtypeStruct((2, 1, fr, 3 * K), BF),
        in_specs=[hbm_spec] * 5,
        out_specs=pl.BlockSpec(memory_space=pltpu.VMEM),
        scratch_shapes=scratch,
        compiler_params=pltpu.CompilerParams(
            collective_id=0, has_side_effects=True, vmem_limit_bytes=GRANT
        ),
    )(*[pltpu.with_memory_space_constraint(a, pltpu.HBM) for a in (leaf, w1, w2, skel1, skel2)])


def solution(mesh):
    return jax.shard_map(
        on_device,
        mesh=mesh,
        in_specs=(
            P(None, None, "box", None, "face", None),
            P(None, None, "box", None),
            P(None, None, "box", None),
            P(),
            P(),
        ),
        out_specs=P(None, None, ("box", "face"), None),
        check_vma=False,
    )
```

time: 51.7 us -> 47.4 us (0.917)
  Pallas kernels: 49.6 us -> 46.5 us
  local copies, waits for them, and re-layouts: 1.77 us -> 0.75 us
    pallas_call x1, Pallas kernels: 49.6 us -> 46.5 us  [on_device(): pl.pallas_call(functools.partial(kernel, fr), out_shape=jax.ShapeDtypeStr...]
    unnamed x1, local copies, waits for them, and re-layouts: 1.77 us -> 0.75 us
where the time goes in v3:
time: 47.4 us; the launch traced here: 47.3 us
  Pallas kernels  46.5 us (98%)
  local copies, waits for them, and re-layouts  0.75 us (2%)
    pallas_call x1, Pallas kernels, on_device(): pl.pallas_call(functools.partial(kernel, fr), out_shape=jax.ShapeDtypeStr...  46.5 us

profile of v3, /device:TPU:1, one launch (start us, length us, event | category | flops | bytes accessed | tf_op | source)
XLA Modules:
  0.0 47.3 jit_solution(14127797521423527671)
XLA Ops:
  0.0 46.5 %shard_map.55 = bf16[2,1,64,1536]{3,2,1,0:T(8,128)(2,1)S(1)} custom-call(bf16[2,1,1,3,64,1536]{5,4,3,2,1,0:T(8,128)(2,1)} %leaf.1, bf16[2,1,256,512]{3,2,1,0:T(8,128)(2,1)} %w1.1, bf16[2,1,128,512]{3,2,1,0:T(8,128)(2,1)} %w2.1, s32[1,16,512]{2,1,0:T(8,128)} %skel1.1, s32[1,8,512]{2,1,0:T(8,128)} %skel2.1), custom_call_target="tpu_custom_call" | custom-call | tf_op jit(solution)/shard_map/pallas_call | solution.py:544
  46.5 0.7 %copy.7 = bf16[2,1,64,1536]{3,2,1,0:T(8,128)(2,1)} copy(bf16[2,1,64,1536]{3,2,1,0:T(8,128)(2,1)S(1)} %shard_map.55) | data formatting | bytes 786432

commit v4 on v3

--- a/solution.py
+++ b/solution.py
@@ -35,16 +35,24 @@
 class Gather:
     def __init__(self, view, send, recv, dsend, drecv, sib):
         self.view, self.send, self.recv, self.dsend, self.drecv, self.sib = view, send, recv, dsend, drecv, sib
-        self.hops, self.hands = [], []
+        self.hops, self.hands, self.split, self.shared = [], [], 8, []
 
     def hop(self, k):
         what, to = self.hops[k]
         ref = self.view(*what)
-        return remote(ref, ref, self.send.at[0], self.recv.at[k], to)
+        return remote(ref, ref, self.send.at[0], self.recv.at[self.sem_of(k)], to)
+
+    def together(self, slots):
+        settle(self.same_bytes(slots, len(slots)), self.recv.at[self.sem_of(slots[0])])
 
     def hand_over(self, k):
         ref = self.view(*self.hands[k])
-        return remote(ref, ref, self.dsend.at[0], self.drecv.at[0], self.sib)
+        return remote(ref, ref, self.dsend.at[0], self.drecv.at[k // self.split], self.sib)
+
+    def sem_of(self, k):
+        first = {slot: group[0] for group in self.shared for slot in group}
+        used = [slot for slot in range(len(self.hops)) if first.get(slot, slot) == slot]
+        return used.index(first.get(k, k))
 
     def got(self, *ks):
         for k in ks:
@@ -98,70 +106,107 @@
         ((far, piece, lo), x),
         ((far, piece, hi), x),
     ]
-    ends, picked, every = (0, 2), (2, 1), (0, 3)
-    g.hands = [
-        (own, every, full),
-        (side, ends, full),
-        (down, every, full),
-        (up, every, full),
-        (side, picked, full),
-        (down_side, every, full),
-        (up_side, every, full),
-        (far, every, full),
-        (far_side, ends, full),
-        (far_side, picked, full),
-    ]
+    ends, picked = (0, 2), (2, 1)
+    places = (own, side, down, up, down_side, up_side, far, far_side)
+    g.shared = [[5, 6], [7, 8], [14, 15], [16, 17], [25, 26]]
+    g.hands = [(place, picked, full) for place in places] + [(place, ends, full) for place in places]
     return g
 
 
-def plane_gather(view, sems, b, f, h, cross_box, sib, fr):
-    g = Gather(view, *sems, sib)
-    y, xh = f // 2, f % 2
-
-    def face(dy, dx):
-        return ((y + dy) % 4) * 2 + (xh + dx) % 2
-
-    xs = [(h, 0), (1 - h, 0), (1 - h, 1), (h, 1)]
-    ys = [0, 1, 3, 2]
-
-    def node(iy, ix):
-        return (xs[ix][0], face(ys[iy], xs[ix][1]))
-
-    alpha, beta = (0, fr // 2), (fr // 2, fr // 2)
-    lo, hi, full = (0, K // 2), (K // 2, K // 2), (0, K)
-    inner, outer = (cross_box, f), (cross_box, face(0, 1))
-    up, down = (b, face(1, 0)), (b, face(3, 0))
-    g.hops += [
-        ((node(0, 0), alpha, full), inner),
-        ((node(0, 0), alpha, full), outer),
-        ((node(0, 1), alpha, lo), outer),
-        ((node(0, 2), alpha, hi), inner),
-    ]
-    g.hops += [
-        ((node(0, 0), beta, full), up),
-        ((node(0, 0), beta, full), down),
-        ((node(2, 0), beta, lo), up),
-        ((node(1, 0), beta, hi), down),
-    ]
-    for i in range(4):
-        g.hops += [
-            ((node(0, i), alpha, full), up),
-            ((node(0, i), alpha, full), down),
-            ((node(2, i), alpha, lo), up),
-            ((node(1, i), alpha, hi), down),
-        ]
-    for i in range(4):
-        g.hops += [
-            ((node(i, 0), beta, full), inner),
-            ((node(i, 0), beta, full), outer),
-            ((node(i, 1), beta, lo), outer),
-            ((node(i, 2), beta, hi), inner),
-        ]
-    g.hands = [(node(i // 2 // 4, i // 2 % 4), (alpha, beta)[i % 2], full) for i in range(32)]
-    return g
-
-
-def kernel(fr, leaf, w1, w2, skel1, skel2, out, sk1v, sk2v, ifs, endr, xs, sel, srow, p1, p2, skt, wa, wb, ga, gt,
+class Plane(Gather):
+    def __init__(self, view, sems, b, f, h, cross_box, sib, fr):
+        super().__init__(view, *sems, sib)
+        self.split = 32
+        y, xh = f // 2, f % 2
+
+        def face(dy, dx):
+            return ((y + dy) % 4) * 2 + (xh + dx) % 2
+
+        xs = [(h, 0), (1 - h, 0), (1 - h, 1), (h, 1)]
+        ys = [0, 1, 3, 2]
+
+        def node(iy, ix):
+            return (xs[ix][0], face(ys[iy], xs[ix][1]))
+
+        lo, hi, full = (0, K // 2), (K // 2, K // 2), (0, K)
+        inner, outer = (cross_box, f), (cross_box, face(0, 1))
+        up, down = (b, face(1, 0)), (b, face(3, 0))
+        for p, piece in enumerate(((0, 0, fr), (1, 0, fr), (2, 0, fr // 2), (2, fr // 2, fr // 2))):
+
+            def line_x():
+                return [(own, inner), (own, outer), (own, (b, face(0, 1)))]
+
+            def line_y():
+                return [(own, up), (own, down), (own, (b, face(2, 0)))]
+
+            def round_x(iy):
+                return [
+                    ((node(iy, 0), piece, full), inner),
+                    ((node(iy, 0), piece, full), outer),
+                    ((node(iy, 1), piece, lo), outer),
+                    ((node(iy, 2), piece, hi), inner),
+                ]
+
+            def round_y(ix):
+                return [
+                    ((node(0, ix), piece, full), up),
+                    ((node(0, ix), piece, full), down),
+                    ((node(2, ix), piece, lo), up),
+                    ((node(1, ix), piece, hi), down),
+                ]
+
+            own = (node(0, 0), piece, full)
+            first, second = (line_x, round_y) if p % 2 == 0 else (line_y, round_x)
+            self.hops += first()
+            for i in range(4):
+                self.hops += second(i)
+            self.hands += [(node(i // 4, i % 4), piece, full) for i in range(16)]
+            k = 19 * p + 5
+            self.shared += [[k, k + 1, k + 4, k + 5, k + 8, k + 9], [k + 12, k + 13]]
+
+    def give(self, p, along, across):
+        iy, ix = (across, along) if p % 2 == 0 else (along, across)
+        self.hand(16 * p + 4 * iy + ix)
+
+    def start(self, p):
+        k = 19 * p
+        self.go(k, k + 1, k + 2, k + 3, k + 4)
+        self.give(p, 0, 0)
+
+    def near(self, p):
+        k = 19 * p
+        for slot in (0, 1):
+            place = 1 + slot if p % 2 == 0 else 2 - slot
+            self.got(k + slot)
+            self.go(k + 3 + 4 * place, k + 4 + 4 * place)
+            self.give(p, place, 0)
+
+    def two_away(self, p):
+        k = 19 * p
+        self.got(k + 2)
+        self.go(k + 15, k + 16)
+        self.give(p, 3, 0)
+
+    def turn(self, p, i):
+        k = 19 * p + 3 + 4 * i
+        for slot in (0, 1):
+            self.got(k + slot)
+            self.go(k + 2 + slot)
+            self.give(p, i, 2 - slot if p % 2 == 0 else 1 + slot)
+
+    def corners(self, p):
+        k = 19 * p + 5
+        self.together([k, k + 1, k + 4, k + 5, k + 8, k + 9])
+        for i in range(3):
+            self.give(p, i, 3)
+
+    def last_corner(self, p):
+        k = 19 * p + 17
+        self.together([k, k + 1])
+        self.give(p, 3, 3)
+
+
+def kernel(fr, leaf, w1, w2, skel1, skel2, out, sk1v, sk2v, ifs, endr, sraw, xs, sel, srow, p1, p2, skt, wa, wb, ga, gt,
            lh, lh2, lhs_s, lh2_s, dp, dps, r2, stg, pex, lsem, ssem, rsem, s1, r1, ds1, dr1, s2, r2s, ds2, dr2,
            asend, arecv, bsend, brecv):
     b, f = lax.axis_index("box"), lax.axis_index("face")
@@ -176,8 +221,8 @@
     not_mid = jnp.logical_not(mid)
 
     barrier = pltpu.get_barrier_semaphore()
-    peers = [(b, f ^ d) for d in range(1, 8)] + [(sib[0], f ^ d) for d in range(8)]
-    peers += [inner, outer, (cross_box, f), (cross_box, other_face)]
+    up, down = (f + 2) % 8, (f + 6) % 8
+    peers = [(b, up), (b, down), (b, other_face), sib, inner, outer, (cross_box, f), (cross_box, other_face)]
     for peer in peers:
         pl.semaphore_signal(barrier, inc=1, device_id=peer, device_id_type=MESH)
 
@@ -204,62 +249,84 @@
     def _():
         pltpu.make_async_copy(chunk_of(f), xs.at[own_rows, :], lsem.at[2]).start()
 
+    sib_rows = pl.ds(pl.multiple_of((1 - c) * K + f * fr, 16), fr)
+
     w1_rows = pl.ds(pl.multiple_of(c * (K // 2), 16), K // 2)
     w2_rows = pl.ds(pl.multiple_of(q * (K // 4), 16), K // 4)
     loc_w1 = local(3, w1.at[:, 0], wa.at[:, w1_rows, :])
     loc_w2 = local(4, w2.at[:, 0], wb.at[:, w2_rows, :])
 
-    loc_s1.wait()
-    loc_s2.wait()
-    sk1 = sk1v[0, pl.ds(b // 2, 1), :]
-    sk2 = sk2v[0, pl.ds(b // 4, 1), :]
-    for part in range(4):
-        at = part * 256
-        index = lax.broadcasted_iota(jnp.int32, (256, K), 0) + at
-        p1[at : at + 256, :] = jnp.where(index == sk1, 1.0, 0.0).astype(BF)
-        p2[at : at + 256, :] = jnp.where(index == sk2, 1.0, 0.0).astype(BF)
-    skt[...] = jnp.transpose(jnp.broadcast_to(sk1.astype(F32), (128, K)))
     loc_ga.wait()
 
     pl.semaphore_wait(barrier, len(peers))
 
     t_if = remote(leaf.at[1 - c, 0, 0, 1 - c, :, 2 * K : 3 * K], ifs.at[c], ssem.at[0], rsem.at[0], sib)
-    t_w1 = remote(w1.at[:, 0], wa.at[:, w1_rows, :], ssem.at[1], rsem.at[1], sib)
-    t_w2 = remote(w2.at[:, 0], wb.at[:, w2_rows, :], ssem.at[2], rsem.at[2], sib)
-    t_w2i = remote(w2.at[0, 0], wb.at[0, w2_rows, :], ssem.at[3], rsem.at[3], inner)
-    t_w2o = remote(w2.at[1, 0], wb.at[1, w2_rows, :], ssem.at[4], rsem.at[4], outer)
+    t_w1 = remote(w1.at[:, 0], wa.at[:, w1_rows, :], ssem.at[0], rsem.at[1], sib)
+    t_w2 = remote(w2.at[:, 0], wb.at[:, w2_rows, :], ssem.at[0], rsem.at[2], sib)
+    t_w2i = remote(w2.at[0, 0], wb.at[0, w2_rows, :], ssem.at[0], rsem.at[3], inner)
+    t_w2o = remote(w2.at[1, 0], wb.at[1, w2_rows, :], ssem.at[0], rsem.at[4], outer)
     q2 = pl.ds(pl.multiple_of((q + 2 - 4 * h) * (K // 4), 16), K // 4)
-    t_w2fi = remote(wb.at[0, q2, :], wb.at[0, q2, :], ssem.at[5], rsem.at[5], sib)
-    t_w2fo = remote(wb.at[1, q2, :], wb.at[1, q2, :], ssem.at[6], rsem.at[6], sib)
-    t_xs = remote(chunk_of(f), xs.at[own_rows, :], ssem.at[7], rsem.at[7], sib)
-    t_pick = remote(stg.at[1 - h], pex, ssem.at[8], rsem.at[8], (cross_box, f))
+    t_w2fi = remote(wb.at[0, q2, :], wb.at[0, q2, :], ssem.at[0], rsem.at[5], sib)
+    t_w2fo = remote(wb.at[1, q2, :], wb.at[1, q2, :], ssem.at[0], rsem.at[6], sib)
+    t_side = remote(leaf.at[:, 0, 0, 2], sraw, ssem.at[1], rsem.at[7], sib)
+    t_pick = remote(stg.at[1 - h], pex, ssem.at[1], rsem.at[8], (cross_box, f))
     picker_box = b - c + h
 
-    def spread_side():
-        for d in (7, 5, 3, 1, 6, 4, 2):
-            remote(chunk_of(f ^ d), xs.at[own_rows, :], asend.at[0], arecv.at[0], (picker_box, f ^ d)).start()
-
+    def sib_chunk_of(j):
+        return sraw.at[j // 4, :, pl.ds(pl.multiple_of(lw * (j % 4), 128), lw)]
+
+    def spread_side(places, first):
+        if first:
+            t_side.wait_recv()
+            pltpu.make_async_copy(sib_chunk_of(f), xs.at[sib_rows, :], lsem.at[5]).start()
+        for d in places:
+            to = (picker_box, f ^ d)
+            remote(chunk_of(f ^ d), xs.at[own_rows, :], asend.at[0], arecv.at[0], to).start()
+            remote(sib_chunk_of(f ^ d), xs.at[sib_rows, :], asend.at[0], arecv.at[0], to).start()
 
     def part_rows(node, blocks, cols):
         rows = pl.ds(pl.multiple_of(node[1] * fr, 16), fr)
         return ga.at[node[0], blocks[0] : blocks[0] + blocks[1], rows, cols[0] : cols[0] + cols[1]]
 
-    def plane_rows(node, rows, cols):
-        at, n = rows
-        return gt.at[node[0], :, pl.ds(pl.multiple_of(node[1] * fr + at, 16), n), cols[0] : cols[0] + cols[1]]
+    def plane_rows(node, piece, cols):
+        block, at, n = piece
+        return gt.at[node[0], block, pl.ds(pl.multiple_of(node[1] * fr + at, 16), n), cols[0] : cols[0] + cols[1]]
+
+    def half_ga(slots, n):
+        return ga.at[0, 0, 0 : n * fr // 2, :]
+
+    def half_gt(slots, n):
+        rows = fr if slots[0] < 38 else fr // 2
+        return gt.at[0, 0, 0 : n * rows // 2, :]
 
     ag1 = face_gather(part_rows, (s1, r1, ds1, dr1), b, f, c, sib)
-    ag2 = plane_gather(plane_rows, (s2, r2s, ds2, dr2), b, f, h, cross_box, sib, fr)
+    ag2 = Plane(plane_rows, (s2, r2s, ds2, dr2), b, f, h, cross_box, sib, fr)
+    ag1.same_bytes, ag2.same_bytes = half_ga, half_gt
 
     t_if.start()
-    ag1.go(18, 19, 0, 1, 2, 20)
+    ag1.go(18, 19, 0)
+    ag1.hand(8)
     t_w1.start()
     t_w2.start()
 
+    @pl.when(mid)
+    def _():
+        t_side.start()
+
+
+    def one_hot(rows, pick):
+        for part in range(4):
+            at = part * 256
+            index = lax.broadcasted_iota(jnp.int32, (256, K), 0) + at
+            pick[at : at + 256, :] = jnp.where(index == rows, 1.0, 0.0).astype(BF)
+
+    loc_s1.wait()
+    sk1 = sk1v[0, pl.ds(b // 2, 1), :]
+    one_hot(sk1, p1)
     loc_if.wait()
     t_if.wait_recv()
     ga[c, 2, face_rows, :] = (fdot(ifs[0], p1[0:K, :]) + fdot(ifs[1], p1[K:, :])).astype(BF)
-    ag1.go(9, 10, 11)
+    ag1.go(9, 10, 11, 1, 2, 20)
     ag1.hand(0)
 
     def coupled(rows, side, left, left2, weights, pick, dest):
@@ -288,63 +355,86 @@
     t_w1.wait_recv()
     coupled(endr, c, lh, lh2, wa, p1, dp)
 
+    skt[...] = jnp.transpose(jnp.broadcast_to(sk1.astype(F32), (128, K)))
+    loc_s2.wait()
+    one_hot(sk2v[0, pl.ds(b // 4, 1), :], p2)
     ag1.got(18)
     ag1.go(21, 23)
     ag1.got(19)
     ag1.go(22, 24)
+    ag1.got(9)
+    ag1.go(12, 13)
+    ag1.hand(1)
+    ag1.got(10)
+    ag1.go(14)
+    ag1.hand(2)
+    ag1.got(11)
+    ag1.go(15)
+    ag1.hand(3)
     ag1.got(0)
     ag1.go(3, 4)
     ag1.got(1)
     ag1.go(5)
+    ag1.hand(10)
     ag1.got(2)
     ag1.go(6)
-    ag1.got(20)
-    ag1.hand(1)
+    ag1.hand(11)
     ag1.got(21)
     ag1.go(25)
     ag1.got(22)
     ag1.go(26)
     t_w2i.start()
     t_w2o.start()
-    ag1.got(9)
-    ag1.go(12, 13)
+    ag1.got(20)
+    ag1.hand(9)
+    ag1.got(12)
+    ag1.go(16)
     ag1.hand(4)
-    ag1.got(10)
-    ag1.go(14)
-    ag1.hand(2)
-    ag1.got(11)
-    ag1.go(15)
-    ag1.hand(3)
+    ag1.got(13)
+    ag1.go(17)
+    ag1.hand(5)
+
+    @pl.when(not_mid)
+    def _():
+        spread_side((7, 5, 3), True)
+
     ag1.got(3)
     ag1.go(7)
     ag1.got(4)
     ag1.go(8)
-    ag1.got(12)
-    ag1.go(16)
-    ag1.got(13)
-    ag1.go(17)
+
+    ag1.got(23)
+    ag1.hand(12)
+    ag1.got(24)
+    ag1.hand(13)
+    ag1.together([14, 15])
+    ag1.hand(6)
+    ag1.together([16, 17])
+    ag1.hand(7)
+
+    @pl.when(not_mid)
+    def _():
+        spread_side((1, 6, 4, 2), False)
 
     @pl.when(mid)
     def _():
-        t_xs.start()
-        spread_side()
-
-    ag1.got(23)
-    ag1.hand(5)
-    ag1.got(24)
-    ag1.hand(6)
-    ag1.got(5, 6, 14, 15)
-    ag1.hand(7)
-    ag1.got(25, 26, 7, 8)
-    ag1.hand(8)
-    ag1.got(16, 17)
-    ag1.hand(9)
+        settle(ga.at[0, 2], dr1.at[0])
+        sides = (base_of(endr, c, dp, 2) - times(lh2, ga, 2)).astype(BF)
+        half = p2[pl.ds(pl.multiple_of(h * K, 16), K), :]
+        stg[...] = fdot(sides, half).astype(BF).reshape(2, fr, K)
+        t_pick.start()
+
+    ag1.together([5, 6])
+    ag1.hand(14)
+    ag1.together([25, 26])
+    ag1.together([7, 8])
+    ag1.hand(15)
 
     @pl.when(not_mid)
     def _():
-        spread_side()
-
-    settle(ga.at[0], dr1.at[0])
+        settle(ga.at[0, 2], dr1.at[0])
+
+    settle(ga.at[0, 0:2], dr1.at[1])
 
     into = srow.at[f // 4, :, pl.ds(pl.multiple_of(lw * (f % 4), 128), lw)]
     dest_box = b - c + 1 - h
@@ -357,7 +447,7 @@
 
     def side_select():
         pltpu.make_async_copy(chunk_of(f), xs.at[own_rows, :], lsem.at[2]).wait()
-        t_xs.wait_recv()
+        pltpu.make_async_copy(sib_chunk_of(f), xs.at[sib_rows, :], lsem.at[5]).wait()
         settle(xs.at[0 : 14 * fr, :], arecv.at[0])
         lane = lax.broadcasted_iota(jnp.int32, (K, 128), 1)
         mine = skt[...].astype(jnp.int32)
@@ -392,44 +482,45 @@
         ag2.go(27 + 4 * i)
         ag2.hand(2 * (4 * i + 2) + 1)
 
+    def finish(block):
+        value = base_of(r2, h, dp, block) - times(lh2, gt, block)
+        out[:, 0, :, block * K : (block + 1) * K] = value.astype(BF).reshape(2, fr, K)
+
     @pl.when(mid)
     def _():
-        sides = (base_of(endr, c, dp, 2) - times(lh2, ga, 2)).astype(BF)
-        half = p2[pl.ds(pl.multiple_of(h * K, 16), K), :]
-        stg[...] = fdot(sides, half).astype(BF).reshape(2, fr, K)
-        t_pick.start()
         ends = fdot(lh2[...], ga[h, 0:2].reshape(2 * K, K))
         gt[h, 0:2, face_rows, :] = (-ends).astype(BF).reshape(2, fr, K)
-        pass_w2()
+        ag2.start(0)
+        ag2.start(1)
         t_pick.wait_recv()
         gt[h, 2, face_rows, :] = stg[h] + pex[...]
-        ag2.go(0, 1, 4, 5, 24, 25, 8, 9)
-        ag2.hand(0, 1)
-        ag2.got(0)
-        ag2.go(2)
-        ag2.got(1)
-        ag2.go(3)
-        ag2.got(4)
-        ag2.go(6)
-        ag2.got(5)
-        ag2.go(7)
-        ag2.go(12, 13, 28, 29, 16, 17, 32, 33)
-        ag2.hand(2, 4, 9, 17)
-        ag2.got(24, 25)
-        ag2.go(26, 27)
-        ag2.got(8, 9)
-        ag2.go(10, 11)
-        ag2.hand(3, 5, 8, 16)
-        ag2.got(2, 3)
-        ag2.go(20, 21)
-        ag2.got(6, 7)
-        ag2.go(36, 37)
-        ag2.hand(6, 25)
-        third(1)
-        ag2.got(26, 27)
-        ag2.got(10, 11)
-        ag2.hand(7, 24)
-
+        ag2.start(2)
+        ag2.start(3)
+        pass_w2()
+        ag2.near(0)
+        ag2.near(1)
+        ag2.turn(0, 0)
+        ag2.turn(1, 0)
+        ag2.near(2)
+        ag2.near(3)
+        ag2.two_away(0)
+        ag2.two_away(1)
+        ag2.turn(2, 0)
+        ag2.turn(3, 0)
+        ag2.turn(0, 1)
+        ag2.turn(1, 1)
+        ag2.two_away(2)
+        ag2.two_away(3)
+        ag2.turn(0, 2)
+        ag2.turn(1, 2)
+
+        ag2.turn(2, 1)
+        ag2.turn(3, 1)
+        ag2.turn(0, 3)
+        ag2.turn(1, 3)
+        for i in (2, 3):
+            ag2.turn(2, i)
+            ag2.turn(3, i)
         settle(srow, brecv.at[0])
         seen = skt[face_rows, :]
         left1 = jnp.tile(jnp.where(seen < K, 1.0, 0.0), (1, 4)).astype(BF)
@@ -451,18 +542,17 @@
             value = base - times(lh2_s, ga, block)
             r2[:, :, block * K : (block + 1) * K] = value.astype(BF).reshape(2, fr, K)
 
-        third(2)
         level_two()
-        third(3)
-        for i in (1, 2):
-            ag2.got(10 + 4 * i, 11 + 4 * i)
-            ag2.hand(2 * (12 + i))
-            ag2.got(26 + 4 * i, 27 + 4 * i)
-            ag2.hand(2 * (4 * i + 3) + 1)
-        ag2.got(22, 23)
-        ag2.hand(30)
-        ag2.got(38, 39)
-        ag2.hand(31)
+        ag2.corners(0)
+        ag2.corners(1)
+        ag2.last_corner(0)
+        ag2.last_corner(1)
+        finish(0)
+        finish(1)
+        ag2.corners(2)
+        ag2.corners(3)
+        ag2.last_corner(2)
+        ag2.last_corner(3)
 
     @pl.when(not_mid)
     def _():
@@ -472,28 +562,27 @@
         pass_w2()
         side_select()
         level_two()
-        settle(gt, dr2.at[0])
-
-    for block in (0, 1, 2):
-        value = base_of(r2, h, dp, block) - times(lh2, gt, block)
-        out[:, 0, :, block * K : (block + 1) * K] = value.astype(BF).reshape(2, fr, K)
-
-    for copy in [t_if, t_w1, t_w2, t_w2i, t_w2o, t_w2fi, t_w2fo]:
-        copy.wait_send()
-    settle(xs.at[0 : 7 * fr, :], asend.at[0])
+        settle(gt.at[:, 0:2], dr2.at[0])
+        finish(0)
+        finish(1)
+        settle(gt.at[:, 2], dr2.at[1])
+
+    finish(2)
+
+    settle(ga.at[0, :, 0 : 7 * fr, :], ssem.at[0])
     settle(ga.at[0, :, 0 : 7 * fr, :], s1.at[0])
     settle(ga.at[0], ds1.at[0])
 
     @pl.when(mid)
     def _():
-        t_xs.wait_send()
-        t_pick.wait_send()
+        settle(ga.at[0, 0, 0 : 7 * fr, :], ssem.at[1])
         settle(gt.at[:, :, 0 : K - fr // 2, :], s2.at[0])
         settle(gt, ds2.at[0])
 
     @pl.when(not_mid)
     def _():
         settle(sel, bsend.at[0])
+        settle(xs.at[0 : 14 * fr, :], asend.at[0])
 
 
 def on_device(leaf, w1, w2, skel1, skel2):
@@ -505,6 +594,7 @@
         pltpu.VMEM(skel1.shape, jnp.int32),
         pltpu.VMEM(skel2.shape, jnp.int32),
         pltpu.VMEM((2, fr, K), BF),
+        pltpu.VMEM((2, fr, 3 * K), BF),
         pltpu.VMEM((2, fr, 3 * K), BF),
         pltpu.VMEM((2 * K, lw), BF),
         pltpu.VMEM((K, lw), BF),
@@ -526,16 +616,16 @@
         pltpu.VMEM((2, fr, K), BF),
         pltpu.VMEM((fr, K), BF),
         dma((8,)),
+        dma((2,)),
         dma((9,)),
-        dma((9,)),
-        dma((1,)),
-        dma((27,)),
-        dma((1,)),
-        dma((1,)),
-        dma((1,)),
-        dma((40,)),
-        dma((1,)),
-        dma((1,)),
+        dma((1,)),
+        dma((22,)),
+        dma((1,)),
+        dma((2,)),
+        dma((1,)),
+        dma((52,)),
+        dma((1,)),
+        dma((2,)),
         dma((1,)),
         dma((1,)),
         dma((1,)),

time: 47.4 us -> 42.5 us (0.90)
  Pallas kernels: 46.5 us -> 41.7 us
    pallas_call x1, Pallas kernels: 46.5 us -> 41.7 us  [on_device(): pl.pallas_call(functools.partial(kernel, fr), out_shape=jax.ShapeDtypeStr...]
where the time goes in v4:
time: 42.5 us; the launch traced here: 42.4 us
  Pallas kernels  41.7 us (98%)
  local copies, waits for them, and re-layouts  0.75 us (2%)
    pallas_call x1, Pallas kernels, on_device(): pl.pallas_call(functools.partial(kernel, fr), out_shape=jax.ShapeDtypeStr...  41.7 us

profile of v4, /device:TPU:1, one launch (start us, length us, event | category | flops | bytes accessed | tf_op | source)
XLA Modules:
  0.0 42.4 jit_solution(12289916927377112103)
XLA Ops:
  0.0 41.7 %shard_map.55 = bf16[2,1,64,1536]{3,2,1,0:T(8,128)(2,1)S(1)} custom-call(bf16[2,1,1,3,64,1536]{5,4,3,2,1,0:T(8,128)(2,1)} %leaf.1, bf16[2,1,256,512]{3,2,1,0:T(8,128)(2,1)} %w1.1, bf16[2,1,128,512]{3,2,1,0:T(8,128)(2,1)} %w2.1, s32[1,16,512]{2,1,0:T(8,128)} %skel1.1, s32[1,8,512]{2,1,0:T(8,128)} %skel2.1), custom_call_target="tpu_custom_call" | custom-call | tf_op jit(solution)/shard_map/pallas_call | solution.py:634
  41.7 0.7 %copy.7 = bf16[2,1,64,1536]{3,2,1,0:T(8,128)(2,1)} copy(bf16[2,1,64,1536]{3,2,1,0:T(8,128)(2,1)S(1)} %shard_map.55) | data formatting | bytes 786432

commit v5 on v4

--- a/solution.py
+++ b/solution.py
@@ -396,7 +396,7 @@
 
     @pl.when(not_mid)
     def _():
-        spread_side((7, 5, 3), True)
+        spread_side((3, 1), True)
 
     ag1.got(3)
     ag1.go(7)
@@ -414,7 +414,7 @@
 
     @pl.when(not_mid)
     def _():
-        spread_side((1, 6, 4, 2), False)
+        spread_side((7, 5, 6, 4, 2), False)
 
     @pl.when(mid)
     def _():

time: 42.5 us -> 41.8 us (0.984)
  Pallas kernels: 41.7 us -> 41 us
    pallas_call x1, Pallas kernels: 41.7 us -> 41 us  [on_device(): pl.pallas_call(functools.partial(kernel, fr), out_shape=jax.ShapeDtypeStr...]
where the time goes in v5:
time: 41.8 us; the launch traced here: 41.7 us
  Pallas kernels  41 us (98%)
  local copies, waits for them, and re-layouts  0.75 us (2%)
    pallas_call x1, Pallas kernels, on_device(): pl.pallas_call(functools.partial(kernel, fr), out_shape=jax.ShapeDtypeStr...  41 us

profile of v5, /device:TPU:1, one launch (start us, length us, event | category | flops | bytes accessed | tf_op | source)
XLA Modules:
  0.0 41.7 jit_solution(8199871924736117083)
XLA Ops:
  0.0 41.0 %shard_map.55 = bf16[2,1,64,1536]{3,2,1,0:T(8,128)(2,1)S(1)} custom-call(bf16[2,1,1,3,64,1536]{5,4,3,2,1,0:T(8,128)(2,1)} %leaf.1, bf16[2,1,256,512]{3,2,1,0:T(8,128)(2,1)} %w1.1, bf16[2,1,128,512]{3,2,1,0:T(8,128)(2,1)} %w2.1, s32[1,16,512]{2,1,0:T(8,128)} %skel1.1, s32[1,8,512]{2,1,0:T(8,128)} %skel2.1), custom_call_target="tpu_custom_call" | custom-call | tf_op jit(solution)/shard_map/pallas_call | solution.py:634
  41.0 0.7 %copy.7 = bf16[2,1,64,1536]{3,2,1,0:T(8,128)(2,1)} copy(bf16[2,1,64,1536]{3,2,1,0:T(8,128)(2,1)S(1)} %shard_map.55) | data formatting | bytes 786432

commit v6 on v5

--- a/solution.py
+++ b/solution.py
@@ -383,8 +383,11 @@
     ag1.go(25)
     ag1.got(22)
     ag1.go(26)
-    t_w2i.start()
-    t_w2o.start()
+
+    @pl.when(not_mid)
+    def _():
+        spread_side((1,), True)
+
     ag1.got(20)
     ag1.hand(9)
     ag1.got(12)
@@ -396,8 +399,10 @@
 
     @pl.when(not_mid)
     def _():
-        spread_side((3, 1), True)
-
+        spread_side((3,), False)
+
+    t_w2i.start()
+    t_w2o.start()
     ag1.got(3)
     ag1.go(7)
     ag1.got(4)

time: 41.8 us -> 41.6 us (level)
  no operation moved by 1% of the time
where the time goes in v6:
time: 41.6 us; the launch traced here: 41.5 us
  Pallas kernels  40.7 us (98%)
  local copies, waits for them, and re-layouts  0.75 us (2%)
    pallas_call x1, Pallas kernels, on_device(): pl.pallas_call(functools.partial(kernel, fr), out_shape=jax.ShapeDtypeStr...  40.7 us

profile of v6, /device:TPU:1, one launch (start us, length us, event | category | flops | bytes accessed | tf_op | source)
XLA Modules:
  0.0 41.5 jit_solution(2549045500422568154)
XLA Ops:
  0.0 40.7 %shard_map.55 = bf16[2,1,64,1536]{3,2,1,0:T(8,128)(2,1)S(1)} custom-call(bf16[2,1,1,3,64,1536]{5,4,3,2,1,0:T(8,128)(2,1)} %leaf.1, bf16[2,1,256,512]{3,2,1,0:T(8,128)(2,1)} %w1.1, bf16[2,1,128,512]{3,2,1,0:T(8,128)(2,1)} %w2.1, s32[1,16,512]{2,1,0:T(8,128)} %skel1.1, s32[1,8,512]{2,1,0:T(8,128)} %skel2.1), custom_call_target="tpu_custom_call" | custom-call | tf_op jit(solution)/shard_map/pallas_call | solution.py:639
  40.8 0.7 %copy.7 = bf16[2,1,64,1536]{3,2,1,0:T(8,128)(2,1)} copy(bf16[2,1,64,1536]{3,2,1,0:T(8,128)(2,1)S(1)} %shard_map.55) | data formatting | bytes 786432

commit v7 on v6

--- a/solution.py
+++ b/solution.py
@@ -408,6 +408,11 @@
     ag1.got(4)
     ag1.go(8)
 
+    @pl.when(not_mid)
+    def _():
+        spread_side((6, 4, 2), False)
+
+
     ag1.got(23)
     ag1.hand(12)
     ag1.got(24)
@@ -419,7 +424,7 @@
 
     @pl.when(not_mid)
     def _():
-        spread_side((7, 5, 6, 4, 2), False)
+        spread_side((7, 5), False)
 
     @pl.when(mid)
     def _():

time: 41.6 us -> 41.5 us (level)
  no operation moved by 1% of the time
where the time goes in v7:
time: 41.5 us; the launch traced here: 41.4 us
  Pallas kernels  40.7 us (98%)
  local copies, waits for them, and re-layouts  0.75 us (2%)
    pallas_call x1, Pallas kernels, on_device(): pl.pallas_call(functools.partial(kernel, fr), out_shape=jax.ShapeDtypeStr...  40.7 us

profile of v7, /device:TPU:1, one launch (start us, length us, event | category | flops | bytes accessed | tf_op | source)
XLA Modules:
  0.0 41.4 jit_solution(5141590641199332142)
XLA Ops:
  0.0 40.7 %shard_map.55 = bf16[2,1,64,1536]{3,2,1,0:T(8,128)(2,1)S(1)} custom-call(bf16[2,1,1,3,64,1536]{5,4,3,2,1,0:T(8,128)(2,1)} %leaf.1, bf16[2,1,256,512]{3,2,1,0:T(8,128)(2,1)} %w1.1, bf16[2,1,128,512]{3,2,1,0:T(8,128)(2,1)} %w2.1, s32[1,16,512]{2,1,0:T(8,128)} %skel1.1, s32[1,8,512]{2,1,0:T(8,128)} %skel2.1), custom_call_target="tpu_custom_call" | custom-call | tf_op jit(solution)/shard_map/pallas_call | solution.py:644
  40.7 0.7 %copy.7 = bf16[2,1,64,1536]{3,2,1,0:T(8,128)(2,1)} copy(bf16[2,1,64,1536]{3,2,1,0:T(8,128)(2,1)S(1)} %shard_map.55) | data formatting | bytes 786432
